TPU v7x, 128 devices: a whole 4x4x4 slice. The times are simulated.
128 devices in a mesh: gauss: 8 (over y, core), tile: 16 (over z, x).
Axes of the slice: x: 4, y: 4, z: 4, core: 2. Of those that a mesh axis runs over, the one named last changes fastest.
Arguments:
- params: float32 [59, 65536], P(None, ('gauss', 'tile')), as said below
- moment_one: float32 [59, 65536], P(None, ('gauss', 'tile')), may hold values from -1.8 to 1.8
- moment_two: float32 [59, 65536], P(None, ('gauss', 'tile')), may hold values from 1e-06 to 0.01
- camera: float32 [3, 11], replicated, as said below
- target: float32 [3, 3, 128, 256], P(None, None, ('gauss', 'tile')), may hold values from 0 to 1
- tile_ids: int32 [3, 128], P(None, ('gauss', 'tile')), may hold values from 0 to 127, as said below
- splat_lists: int32 [3, 128, 256], P(None, ('gauss', 'tile')), may hold values from 0 to 65535, as said below
- counts: int32 [3, 128], P(None, ('gauss', 'tile')), may hold values from 32 to 256, as said below
Outputs:
- new_params: float32 [59, 65536], P(None, ('gauss', 'tile'))
- new_first: float32 [59, 65536], P(None, ('gauss', 'tile'))
- new_second: float32 [59, 65536], P(None, ('gauss', 'tile'))
- rendered: float32 [3, 3, 128, 256], P(None, None, ('gauss', 'tile'))
- view_losses: float32 [3], replicated
Inputs may be any that keep to these rules, and one draw needn't show every extreme that they name: `splat_lists`: entries of slot q lie in [b * 8192, (b + 1) * 8192) with b = q // 16; entries at or past the slot's count are padding. `counts`: every view has a slot whose count is 256. `tile_ids`: in each view the slots q with q // 16 = b hold each tile of b * 16 to (b + 1) * 16 - 1 once. `params`: row 6 lies in [0.5, 1.5]. `camera`: entries 8 to 10 of each row form a unit vector.
All inputs are finite; a program needn't handle non-finite values.
Results may differ from a plain program's by a relative error of at most 0.0003.
Values sent between devices are 32-bit elements; how exact they have to be, the bound alone decides.
No kernel may reach another device: no remote copies, remote signals or barrier semaphores. Data moves between devices by JAX's collectives and lax.ppermute only.
A program may use at most 64 MiB of HBM per device.

v0:
```python
import jax
import jax.numpy as jnp
from jax import lax
from jax.experimental import pallas as pl
from jax.experimental.pallas import tpu as pltpu
from jax.sharding import Mesh
from jax.sharding import PartitionSpec as P

VIEWS = 3
TILES_WIDE = 4
TILE = ("tile_0", "tile_1")
GAUSS_TILE = ("gauss_0", "gauss_1", "tile_0", "tile_1")
OWNERS = 16
OWN = 512
GEOMETRY = 11
ROWS = 20
SEND = 4 * ROWS
BACK = SEND + 8
GROUPS = 6
LOG2E = 1.4426950408889634

band_zero = 0.28209479177387814
band_one = 0.4886025119029199
band_two = (
    1.0925484305920792,
    -1.0925484305920792,
    0.31539156525252005,
    -1.0925484305920792,
    0.5462742152960396,
)
band_three = (
    -0.5900435899266435,
    2.890611442640554,
    -0.4570457994644658,
    0.3731763325901154,
    -0.4570457994644658,
    1.445305721320277,
    -0.5900435899266435,
)

f32 = jnp.float32
bf16 = jnp.bfloat16


def iota(shape, dim):
    return lax.broadcasted_iota(jnp.int32, shape, dim)


def harmonic_halves(camera_ref, view):
    x, y, z = [jnp.full((8, 128), camera_ref[view, 8 + i], f32) for i in range(3)]
    xx, yy, zz = x * x, y * y, z * z
    values = [
        jnp.full((8, 128), band_zero, f32),
        -band_one * y,
        band_one * z,
        -band_one * x,
        band_two[0] * x * y,
        band_two[1] * y * z,
        band_two[2] * (2.0 * zz - xx - yy),
        band_two[3] * x * z,
        band_two[4] * (xx - yy),
        band_three[0] * y * (3.0 * xx - yy),
        band_three[1] * x * y * z,
        band_three[2] * y * (4.0 * zz - xx - yy),
        band_three[3] * z * (2.0 * zz - 3.0 * xx - 3.0 * yy),
        band_three[4] * x * (4.0 * zz - xx - yy),
        band_three[5] * z * (xx - yy),
        band_three[6] * x * (xx - 3.0 * yy),
    ]
    row = iota((8, 128), 0)
    halves = []
    for half in range(2):
        column = values[8 * half]
        for i in range(1, 8):
            column = jnp.where(row == i, values[8 * half + i], column)
        halves.append(column)
    return halves


def pack_kernel(params_ref, camera_ref, send_ref, slope_ref, pack_ref, tall_ref):
    for quarter in range(4):
        lanes = pl.ds(128 * quarter, 128)
        pack_ref[pl.ds(quarter, 8, stride=4), :] = params_ref[0:8, lanes]
        pack_ref[pl.ds(32 + quarter, 3, stride=4), :] = params_ref[8:11, lanes]
        tall_ref[pl.ds(64 * quarter, 59), :] = params_ref[:, lanes]
    columns = [harmonic_halves(camera_ref, view) for view in range(VIEWS)]
    for k in range(3):
        for quarter in range(4):
            low = tall_ref[pl.ds(64 * quarter + 11 + k, 8, stride=3), :]
            high = tall_ref[pl.ds(64 * quarter + 35 + k, 8, stride=3), :]
            for view in range(VIEWS):
                terms = columns[view][0] * low + columns[view][1] * high
                raw = jnp.sum(terms, axis=0, keepdims=True) + 0.5
                row = 4 * (3 * view + k) + quarter
                pack_ref[pl.ds(4 * GEOMETRY + row, 1), :] = jnp.maximum(raw, 0.0)
                slope_ref[pl.ds(row, 1), :] = jnp.where(
                    raw > 0.0, 1.0, jnp.where(raw == 0.0, 0.5, 0.0)
                )
    packed = pack_ref[...]
    for owner in range(OWNERS):
        send_ref[pl.ds(SEND * owner, SEND), :] = packed


def split(value):
    high = value.astype(bf16)
    return high, (value - high.astype(f32)).astype(bf16)


def nn(lhs, rhs):
    return lax.dot_general(lhs, rhs, (((1,), (0,)), ((), ())), preferred_element_type=f32)


def nt(lhs, rhs):
    return lax.dot_general(lhs, rhs, (((1,), (1,)), ((), ())), preferred_element_type=f32)


def tn(lhs, rhs):
    return lax.dot_general(lhs, rhs, (((0,), (0,)), ((), ())), preferred_element_type=f32)


def render_kernel(
    table_ref,
    lists_ref,
    counts_ref,
    tiles_ref,
    camera_ref,
    target_ref,
    rendered_ref,
    back_ref,
    found_ref,
    lane_ref,
    rows_ref,
    colour_ref,
    shade_ref,
    logs_ref,
    keep_ref,
    high_ref,
    low_ref,
    moment_ref,
    tint_ref,
    grads_ref,
    spread_ref,
    places_ref,
    tri_ref,
    loss_ref,
):
    quarter = iota((8, 128), 0) & 3
    for group in range(GROUPS):
        view, half = divmod(group, 2)
        local = lists_ref[view, :, 128 * half : 128 * half + 128] & 8191
        local = jnp.broadcast_to(local, (8, 128))
        lane = local & 127
        block = (local >> 7) - quarter
        first = (4 * (GEOMETRY + 3 * view)) // 8
        last = (4 * (GEOMETRY + 3 * view + 3) - 1) // 8
        pieces = sorted(set(range(6)) | set(range(first, last + 1)))
        found = {piece: jnp.zeros((8, 128), f32) for piece in pieces}
        for owner in range(OWNERS):
            here = block == 4 * owner
            for piece in pieces:
                rows = table_ref[pl.ds(SEND * owner + 8 * piece, 8), :]
                picked = jnp.take_along_axis(rows, lane, axis=1, mode="promise_in_bounds")
                found[piece] = jnp.where(here, picked, found[piece])
        for piece in pieces:
            found_ref[pl.ds(SEND * group + 8 * piece, 8), :] = found[piece]

    def entry_row(row):
        parts = [found_ref[pl.ds(4 * row + q, GROUPS, stride=SEND), :] for q in range(4)]
        return (parts[0] + parts[1]) + (parts[2] + parts[3])

    for group in range(GROUPS):
        view, half = divmod(group, 2)
        for k in range(3):
            start = SEND * group + 4 * (GEOMETRY + 3 * view + k)
            value = jnp.sum(found_ref[pl.ds(start, 4), :], axis=0, keepdims=True)
            colour_ref[pl.ds(8 * view + k, 1), pl.ds(128 * half, 128)] = value

    place = iota((GROUPS, 128), 0)

    def per_view(values):
        return jnp.where(place < 2, values[0], jnp.where(place < 4, values[1], values[2]))

    camera = [per_view([camera_ref[view, i] for view in range(VIEWS)]) for i in range(8)]
    affine = (camera[0:3], camera[3:6])
    centre = [entry_row(i) for i in range(3)]
    scale = [jnp.exp(entry_row(3 + i)) for i in range(3)]
    raw = [entry_row(6 + i) for i in range(4)]
    logit = entry_row(10)
    inverse_norm = 1.0 / jnp.sqrt(
        raw[0] * raw[0] + raw[1] * raw[1] + raw[2] * raw[2] + raw[3] * raw[3]
    )
    qw, qx, qy, qz = [component * inverse_norm for component in raw]
    rotation = [
        [1.0 - 2.0 * (qy * qy + qz * qz), 2.0 * (qx * qy - qw * qz), 2.0 * (qx * qz + qw * qy)],
        [2.0 * (qx * qy + qw * qz), 1.0 - 2.0 * (qx * qx + qz * qz), 2.0 * (qy * qz - qw * qx)],
        [2.0 * (qx * qz - qw * qy), 2.0 * (qy * qz + qw * qx), 1.0 - 2.0 * (qx * qx + qy * qy)],
    ]
    stretched = [[rotation[i][j] * scale[j] for j in range(3)] for i in range(3)]
    screen = [
        [sum(affine[k][i] * stretched[i][j] for i in range(3)) for j in range(3)] for k in range(2)
    ]
    cov_a = sum(screen[0][j] * screen[0][j] for j in range(3)) + 0.3
    cov_b = sum(screen[0][j] * screen[1][j] for j in range(3))
    cov_c = sum(screen[1][j] * screen[1][j] for j in range(3)) + 0.3
    inverse_det = 1.0 / (cov_a * cov_c - cov_b * cov_b)
    position = (place & 1) * 128 + iota((GROUPS, 128), 1)
    live = position < per_view([counts_ref[view, 0] for view in range(VIEWS)])
    conic = [
        jnp.where(live, value * inverse_det, 0.0) for value in (cov_c, -cov_b, cov_a)
    ]
    mean = [sum(affine[k][i] * centre[i] for i in range(3)) + camera[6 + k] for k in range(2)]
    opacity = 1.0 / (1.0 + jnp.exp(-logit))
    shown = jnp.where(live, opacity, 0.0)
    tile = per_view([tiles_ref[view, 0] for view in range(VIEWS)])
    middle_x = (tile % TILES_WIDE * 16 + 8).astype(f32)
    middle_y = (tile // TILES_WIDE * 16 + 8).astype(f32)
    shift_x = mean[0] - middle_x
    shift_y = mean[1] - middle_y
    quantities = [
        shift_x,
        shift_y,
        (-0.5 * LOG2E) * conic[0],
        (-LOG2E) * conic[1],
        (-0.5 * LOG2E) * conic[2],
        shown,
    ]
    for n, value in enumerate(quantities):
        lane_ref[pl.ds(8 * n, GROUPS), :] = value
    for n in range(len(quantities)):
        for half in range(2):
            rows_ref[pl.ds(8 * n, VIEWS), pl.ds(128 * half, 128)] = lane_ref[
                pl.ds(8 * n + half, VIEWS, stride=2), :
            ]

    before = iota((256, 256), 0)
    after = iota((256, 256), 1)
    strictly = jnp.where(before < after, 1.0, 0.0).astype(bf16)
    tri_ref[0:256, :] = strictly
    tri_ref[256:512, :] = strictly
    strictly = jnp.where(before > after, 1.0, 0.0).astype(bf16)
    tri_ref[512:768, :] = strictly
    tri_ref[768:1024, :] = strictly
    pixel = iota((16, 256), 1)
    power = iota((16, 256), 0)
    pixel_u = (pixel % 16).astype(f32) - 7.5
    pixel_v = (pixel // 16).astype(f32) - 7.5
    basis = jnp.where(power == 0, 1.0, jnp.where(power == 1, pixel_u, pixel_v))
    basis = jnp.where(power == 3, pixel_u * pixel_u, basis)
    basis = jnp.where(power == 4, pixel_u * pixel_v, basis)
    basis = jnp.where(power == 5, pixel_v * pixel_v, basis)
    basis = jnp.where(power > 5, 0.0, basis).astype(bf16)
    offset = iota((16, 256), 0).astype(f32) - 7.5
    loss_ref[...] = jnp.zeros_like(loss_ref)
    kinds = iota((16, 256), 0)

    def one_view(view, carry):
        def row(n):
            return rows_ref[pl.ds(8 * n + view, 1), :]

        mean_u, mean_v = row(0), row(1)
        opaque = jnp.broadcast_to(row(5), (16, 256))
        dx = offset - mean_u
        along = row(2) * dx * dx
        across = row(3) * dx
        upright = row(4)
        for line in range(16):
            dy = (line - 7.5) - mean_v
            exponent = along + (upright * dy * dy + across * dy)
            shade = opaque * jnp.exp2(exponent)
            shade_ref[pl.ds(16 * line, 16), :] = shade
            high, low = split(jnp.log(1.0 - jnp.minimum(shade, 0.99)))
            logs_ref[pl.ds(16 * line, 16), 0:256] = high
            logs_ref[pl.ds(16 * line, 16), 256:512] = low
        for part in range(4):
            rows = pl.ds(64 * part, 64)
            keep = jnp.exp(nn(logs_ref[rows, :], tri_ref[0:512, :]))
            keep_ref[rows, :] = keep
            high, low = split(jnp.minimum(shade_ref[rows, :], 0.99) * keep)
            high_ref[rows, :] = high
            low_ref[rows, :] = low
        colour = colour_ref[pl.ds(pl.multiple_of(8 * view, 8), 8), :]
        colour_high, colour_low = [part.astype(f32) for part in split(colour)]
        stacked = jnp.concatenate(
            [
                colour_high[0:3],
                colour_high[0:3],
                colour_low[0:3],
                jnp.zeros((7, 256), f32),
            ],
            axis=0,
        ).astype(bf16)
        image_high = nt(stacked, high_ref[...])
        image_low = nt(stacked, low_ref[...])
        image = image_high[0:3] + image_high[6:9] + image_low[0:3]
        residuals = []
        total = jnp.zeros((1, 256), f32)
        for k in range(3):
            rendered_ref[view, k, :, :] = image[k : k + 1]
            residual = image[k : k + 1] - target_ref[view, k, :, :]
            total = total + residual * residual
            residuals.append(residual * (1.0 / (VIEWS * 256)))
        loss_ref[...] += jnp.where(
            iota((8, 128), 1) == view, jnp.sum(total, axis=1, keepdims=True), 0.0
        )
        error = jnp.concatenate(residuals, axis=0)
        error_high, error_low = [part.astype(f32) for part in split(error)]
        pulled = jnp.concatenate(
            [error_high, error_low, error_high, jnp.zeros((7, 256), f32)], axis=0
        ).astype(bf16)
        tint = nn(pulled, high_ref[...])
        tint_low = nn(pulled, low_ref[...])
        tint_ref[pl.ds(pl.multiple_of(8 * view, 8), 3), :] = (
            tint[0:3] + tint[3:6] + tint_low[0:3]
        )
        pull = tn(pulled, stacked)
        for part in range(4):
            rows = pl.ds(64 * part, 64)
            weight = jnp.minimum(shade_ref[rows, :], 0.99) * keep_ref[rows, :]
            high, low = split(pull[64 * part : 64 * part + 64] * weight)
            logs_ref[rows, 0:256] = high
            logs_ref[rows, 256:512] = low
        for part in range(4):
            rows = pl.ds(64 * part, 64)
            behind = nn(logs_ref[rows, :], tri_ref[512:1024, :])
            shade = shade_ref[rows, :]
            alpha = jnp.minimum(shade, 0.99)
            slope = pull[64 * part : 64 * part + 64] * keep_ref[rows, :] - behind / (1.0 - alpha)
            passed = jnp.where(shade < 0.99, shade, jnp.where(shade == 0.99, 0.5 * shade, 0.0))
            high, low = split(slope * passed)
            high_ref[rows, :] = high
            low_ref[rows, :] = low
        moments = nn(basis, high_ref[...]) + nn(basis, low_ref[...])
        for half in range(2):
            moment_ref[pl.ds(2 * view + half, 8, stride=8), :] = moments[
                0:8, 128 * half : 128 * half + 128
            ]
        return carry

    lax.fori_loop(0, VIEWS, one_view, 0)

    m_0, m_u, m_v, m_uu, m_uv, m_vv = [
        moment_ref[pl.ds(8 * n, GROUPS), :] for n in range(6)
    ]
    m_x = m_u - shift_x * m_0
    m_y = m_v - shift_y * m_0
    m_xx = m_uu - 2.0 * shift_x * m_u + shift_x * shift_x * m_0
    m_xy = m_uv - shift_x * m_v - shift_y * m_u + shift_x * shift_y * m_0
    m_yy = m_vv - 2.0 * shift_y * m_v + shift_y * shift_y * m_0
    d_mean = (conic[0] * m_x + conic[1] * m_y, conic[1] * m_x + conic[2] * m_y)
    left = (
        (conic[0] * m_xx + conic[1] * m_xy, conic[0] * m_xy + conic[1] * m_yy),
        (conic[1] * m_xx + conic[2] * m_xy, conic[1] * m_xy + conic[2] * m_yy),
    )
    d_a = 0.5 * (left[0][0] * conic[0] + left[0][1] * conic[1])
    d_b = left[0][0] * conic[1] + left[0][1] * conic[2]
    d_c = 0.5 * (left[1][0] * conic[1] + left[1][1] * conic[2])
    d_screen = [
        [2.0 * d_a * screen[0][j] + d_b * screen[1][j] for j in range(3)],
        [2.0 * d_c * screen[1][j] + d_b * screen[0][j] for j in range(3)],
    ]
    d_stretched = [
        [affine[0][i] * d_screen[0][j] + affine[1][i] * d_screen[1][j] for j in range(3)]
        for i in range(3)
    ]
    d_scale = [sum(d_stretched[i][j] * stretched[i][j] for i in range(3)) for j in range(3)]
    r = [[d_stretched[i][j] * scale[j] for j in range(3)] for i in range(3)]
    d_unit = [
        2.0 * (qz * (r[1][0] - r[0][1]) + qy * (r[0][2] - r[2][0]) + qx * (r[2][1] - r[1][2])),
        2.0
        * (
            qy * (r[0][1] + r[1][0])
            + qz * (r[0][2] + r[2][0])
            + qw * (r[2][1] - r[1][2])
            - 2.0 * qx * (r[1][1] + r[2][2])
        ),
        2.0
        * (
            qx * (r[0][1] + r[1][0])
            + qz * (r[1][2] + r[2][1])
            + qw * (r[0][2] - r[2][0])
            - 2.0 * qy * (r[0][0] + r[2][2])
        ),
        2.0
        * (
            qx * (r[0][2] + r[2][0])
            + qy * (r[1][2] + r[2][1])
            + qw * (r[1][0] - r[0][1])
            - 2.0 * qz * (r[0][0] + r[1][1])
        ),
    ]
    unit = (qw, qx, qy, qz)
    radial = sum(unit[i] * d_unit[i] for i in range(4))
    gradients = (
        [affine[0][i] * d_mean[0] + affine[1][i] * d_mean[1] for i in range(3)]
        + d_scale
        + [(d_unit[i] - unit[i] * radial) * inverse_norm for i in range(4)]
        + [m_0 * (1.0 - opacity)]
    )
    for n, value in enumerate(gradients):
        high = value.astype(bf16).astype(f32)
        grads_ref[pl.ds(16 * n, GROUPS), :] = high
        grads_ref[pl.ds(16 * n + 8, GROUPS), :] = value - high

    coarse = iota((32, 128), 0)
    fine = iota((256, 128), 0)
    kinds_of = GEOMETRY * 32
    for group in range(GROUPS):
        view, half = divmod(group, 2)
        local = lists_ref[view, :, 128 * half : 128 * half + 128] & 8191
        lanes = pl.ds(128 * group, 128)
        places_ref[:, lanes] = jnp.where((local & 255) == fine, 1.0, 0.0).astype(bf16)
        owner_part = ((local >> 8) & 1) * 16 + (local >> 9)
        chosen = jnp.where(owner_part == coarse, 1.0, 0.0).astype(bf16)
        for n in range(GEOMETRY):
            for part in range(2):
                value = grads_ref[pl.ds(16 * n + 8 * part + group, 1), :]
                spread_ref[pl.ds(kinds_of * part + 32 * n, 32), lanes] = (
                    chosen * jnp.broadcast_to(value, (32, 128)).astype(bf16)
                )
        for k in range(3):
            value = tint_ref[pl.ds(8 * view + k, 1), pl.ds(128 * half, 128)]
            high = value.astype(bf16).astype(f32)
            for part, piece in enumerate((high, value - high)):
                spread_ref[pl.ds(2 * kinds_of + 96 * part + 32 * k, 32), lanes] = (
                    chosen * jnp.broadcast_to(piece, (32, 128)).astype(bf16)
                )

    def store(row, value):
        for upper in range(2):
            for side in range(2):
                back_ref[pl.ds(4 * row + 2 * upper + side, 16, stride=BACK), :] = value[
                    16 * upper : 16 * upper + 16, 128 * side : 128 * side + 128
                ]

    dense = nt(spread_ref[0 : 2 * kinds_of, :], places_ref[...])
    for n in range(GEOMETRY):
        store(n, dense[32 * n : 32 * n + 32] + dense[kinds_of + 32 * n : kinds_of + 32 * n + 32])
    for view in range(VIEWS):
        lanes = slice(256 * view, 256 * view + 256)
        dense = nt(spread_ref[2 * kinds_of : 2 * kinds_of + 192, lanes], places_ref[:, lanes])
        for k in range(3):
            store(
                GEOMETRY + 3 * view + k,
                dense[32 * k : 32 * k + 32] + dense[96 + 32 * k : 96 + 32 * k + 32],
            )
    for owner in range(OWNERS):
        back_ref[pl.ds(BACK * owner + SEND, 8), :] = loss_ref[...]


def adam_kernel(
    back_ref,
    slope_ref,
    params_ref,
    moment_one_ref,
    moment_two_ref,
    camera_ref,
    params_out,
    first_out,
    second_out,
    loss_out,
    total_ref,
    gradient_ref,
):
    total = back_ref[0:BACK, :]
    for owner in range(1, OWNERS):
        total = total + back_ref[pl.ds(BACK * owner, BACK), :]
    total_ref[...] = total
    loss_out[...] = total[SEND : SEND + 8]
    columns = [harmonic_halves(camera_ref, view) for view in range(VIEWS)]
    row = iota((59, 128), 0)
    rates = jnp.where(row < 14, 0.0025, 0.000125)
    rates = jnp.where(row < 11, 0.05, rates)
    rates = jnp.where(row < 10, 0.001, rates)
    rates = jnp.where(row < 6, 0.005, rates)
    rates = jnp.where(row < 3, 0.00016, rates)
    for quarter in range(4):
        lanes = pl.ds(128 * quarter, 128)
        base = 64 * quarter
        gradient_ref[pl.ds(base, 8), :] = total_ref[pl.ds(quarter, 8, stride=4), :]
        gradient_ref[pl.ds(base + 8, 3), :] = total_ref[pl.ds(32 + quarter, 3, stride=4), :]
        for k in range(3):
            tints = []
            for view in range(VIEWS):
                row = 4 * (3 * view + k) + quarter
                tint = total_ref[pl.ds(4 * GEOMETRY + row, 1), :] * slope_ref[pl.ds(row, 1), :]
                tints.append(jnp.broadcast_to(tint, (8, 128)))
            for half in range(2):
                gradient_ref[pl.ds(base + 11 + 24 * half + k, 8, stride=3), :] = sum(
                    columns[view][half] * tints[view] for view in range(VIEWS)
                )
        gradient = gradient_ref[pl.ds(base, 59), :]
        first = 0.9 * moment_one_ref[:, lanes] + 0.1 * gradient
        second = 0.999 * moment_two_ref[:, lanes] + 0.001 * gradient * gradient
        first_out[:, lanes] = first
        second_out[:, lanes] = second
        params_out[:, lanes] = params_ref[:, lanes] - rates * first / (jnp.sqrt(second) + 1e-15)


VM = pl.BlockSpec(memory_space=pltpu.VMEM)
SM = pl.BlockSpec(memory_space=pltpu.SMEM)


def shape(*dims):
    return jax.ShapeDtypeStruct(dims, f32)


def over_pairs(value, axis, pairs):
    both = [(a, b) for a, b in pairs] + [(b, a) for a, b in pairs]
    return value + lax.ppermute(value, axis, both)


def shards(params, moment_one, moment_two, camera, target, tile_ids, splat_lists, counts):
    sent, slope = pl.pallas_call(
        pack_kernel,
        out_shape=(shape(OWNERS * SEND, 128), shape(36, 128)),
        in_specs=[VM, SM],
        out_specs=(VM, VM),
        scratch_shapes=[pltpu.VMEM((SEND, 128), f32), pltpu.VMEM((256, 128), f32)],
        name="pack",
    )(params, camera)
    table = lax.all_to_all(
        sent.reshape(OWNERS, SEND, 128), TILE, split_axis=0, concat_axis=0, tiled=True
    ).reshape(OWNERS * SEND, 128)
    rendered, back = pl.pallas_call(
        render_kernel,
        out_shape=(shape(VIEWS, 3, 1, 256), shape(OWNERS * BACK, 128)),
        in_specs=[VM, VM, SM, SM, SM, VM],
        out_specs=(VM, VM),
        scratch_shapes=[
            pltpu.VMEM((GROUPS * SEND, 128), f32),
            pltpu.VMEM((48, 128), f32),
            pltpu.VMEM((48, 256), f32),
            pltpu.VMEM((24, 256), f32),
            pltpu.VMEM((256, 256), f32),
            pltpu.VMEM((256, 512), bf16),
            pltpu.VMEM((256, 256), f32),
            pltpu.VMEM((256, 256), bf16),
            pltpu.VMEM((256, 256), bf16),
            pltpu.VMEM((64, 128), f32),
            pltpu.VMEM((24, 256), f32),
            pltpu.VMEM((16 * GEOMETRY, 128), f32),
            pltpu.VMEM((2 * 32 * GEOMETRY + 192, 768), bf16),
            pltpu.VMEM((256, 768), bf16),
            pltpu.VMEM((1024, 256), bf16),
            pltpu.VMEM((8, 128), f32),
        ],
        name="render",
    )(table, splat_lists, counts, tile_ids, camera, target)
    arrived = lax.all_to_all(
        back.reshape(OWNERS, BACK, 128), TILE, split_axis=0, concat_axis=0, tiled=True
    ).reshape(OWNERS * BACK, 128)
    updated, first, second, loss = pl.pallas_call(
        adam_kernel,
        out_shape=(shape(59, 512), shape(59, 512), shape(59, 512), shape(8, 128)),
        in_specs=[VM, VM, VM, VM, VM, SM],
        out_specs=(VM, VM, VM, VM),
        scratch_shapes=[pltpu.VMEM((BACK, 128), f32), pltpu.VMEM((256, 128), f32)],
        name="adam",
    )(arrived, slope, params, moment_one, moment_two, camera)
    loss = over_pairs(loss, "gauss_1", [(0, 1)])
    loss = over_pairs(loss, "gauss_0", [(0, 1), (2, 3)])
    loss = over_pairs(loss, "gauss_0", [(0, 3), (1, 2)])
    return (updated, first, second, rendered, loss[0, :VIEWS] * (0.5 / (3 * 256 * 128)))


def solution(mesh):
    finer = Mesh(mesh.devices.reshape(4, 2, 4, 4), GAUSS_TILE)
    in_specs = (
        P(None, GAUSS_TILE),
        P(None, GAUSS_TILE),
        P(None, GAUSS_TILE),
        P(),
        P(None, None, GAUSS_TILE, None),
        P(None, GAUSS_TILE),
        P(None, GAUSS_TILE, None),
        P(None, GAUSS_TILE),
    )
    out_specs = (
        P(None, GAUSS_TILE),
        P(None, GAUSS_TILE),
        P(None, GAUSS_TILE),
        P(None, None, GAUSS_TILE, None),
        P(),
    )
    return jax.shard_map(
        shards, mesh=finer, in_specs=in_specs, out_specs=out_specs, check_vma=False
    )
```

profile of v0, /device:TPU:0, one launch (start us, length us, event | category | flops | bytes accessed | tf_op | source)
XLA Modules:
  0.0 61.2 jit_solution(2513986202731414117)
XLA Ops:
  0.6 1.9 %pack.1 = (f32[1280,128]{1,0:T(8,128)}, f32[36,128]{1,0:T(8,128)}) custom-call(f32[59,512]{1,0:T(8,128)} %params_ref.3, f32[3,11]{1,0:T(4,128)} %camera_ref.5), custom_call_target="tpu_custom_call" | custom-call | tf_op jit(solution)/shard_map/pack/pallas_call | solution.py:513
  2.5 0.0 copy-start.1
  2.5 8.1 %all-to-all-start = ((f32[16,80,128]{2,1,0:T(8,128)}), f32[16,80,128]{2,1,0:T(8,128)S(1)}, u32[]{:S(2)}, u32[]{:S(2)}) async-start(f32[16,80,128]{2,1,0:T(8,128)} %bitcast.9), calls=%async_computation | async-start | bytes 1310720 | tf_op jit(solution)/shard_map/all_to_all | solution.py:521
  10.7 0.0 copy-done.1
  10.7 0.0 copy-start.2
  10.7 0.7 %copy.14.tiles_ref = s32[3,1]{1,0:T(4,128)} copy(s32[3,1]{0,1:T(1,128)S(1)} %copy-done.1) | data formatting | bytes 24 | tf_op args[5]
  11.3 0.0 copy-done.2
  11.3 0.7 %copy.13.counts_ref = s32[3,1]{1,0:T(4,128)} copy(s32[3,1]{0,1:T(1,128)S(1)} %copy-done.2) | data formatting | bytes 24 | tf_op args[7]
  12.0 11.6 %all-to-all-done = f32[16,80,128]{2,1,0:T(8,128)S(1)} async-done(((f32[16,80,128]{2,1,0:T(8,128)}), f32[16,80,128]{2,1,0:T(8,128)S(1)}, u32[]{:S(2)}, u32[]{:S(2)}) %all-to-all-start) | async-done | bytes 655392 | tf_op jit(solution)/shard_map/all_to_all | solution.py:521
  23.6 0.0 copy-start
  23.6 0.8 %copy-done = f32[16,80,128]{2,1,0:T(8,128)} copy-done((f32[16,80,128]{2,1,0:T(8,128)}, f32[16,80,128]{2,1,0:T(8,128)S(1)}, u32[]{:S(2)}) %copy-start) | copy-done | bytes 655384
  24.4 6.8 %render.1 = (f32[3,3,1,256]{3,2,1,0:T(1,128)}, f32[1408,128]{1,0:T(8,128)}) custom-call(f32[1280,128]{1,0:T(8,128)} %bitcast.7, s32[3,1,256]{2,1,0:T(1,128)} %lists_ref.1, s32[3,1]{1,0:T(4,128)} %copy.13.counts_ref, s32[3,1]{1,0:T(4,128)} %copy.14.tiles_ref, f32[3,11]{1,0:T(4,128)} %camera_ref.5, f32[3,3,1,256]{3,2,1,0:T(1,128)} %target_ref.1), custom_call_target="tpu_custom_call" | custom-call | tf_op jit(solution)/shard_map/render/pallas_call | solution.py:524
  31.2 16.8 %all_to_all.10 = f32[16,88,128]{2,1,0:T(8,128)} all-to-all(f32[16,88,128]{2,1,0:T(8,128)} %bitcast.8), channel_id=1, replica_groups=mesh['gauss_0'=4,'gauss_1'=2,'tile_0'=4,'tile_1'=4] {'tile_0','tile_1'}, dimensions={0} | all-to-all | bytes 1441792 | tf_op jit(solution)/shard_map/all_to_all | solution.py:549
  48.0 2.1 %adam.1 = (f32[59,512]{1,0:T(8,128)}, f32[59,512]{1,0:T(8,128)}, f32[59,512]{1,0:T(8,128)}, f32[8,128]{1,0:T(8,128)}) custom-call(f32[1408,128]{1,0:T(8,128)} %bitcast.6, f32[36,128]{1,0:T(8,128)} %get-tuple-element.15.slope_ref, f32[59,512]{1,0:T(8,128)} %params_ref.3, f32[59,512]{1,0:T(8,128)} %moment_one_ref.1, f32[59,512]{1,0:T(8,128)} %moment_two_ref.1, ...), custom_call_target="tpu_custom_call" | custom-call | tf_op jit(solution)/shard_map/adam/pallas_call | solution.py:552
  50.2 0.0 collective-permute-start
  50.2 1.4 %collective-permute-done = f32[8,128]{1,0:T(8,128)S(1)} collective-permute-done((f32[8,128]{1,0:T(8,128)}, f32[8,128]{1,0:T(8,128)S(1)}, u32[]{:S(2)}, u32[]{:S(2)}) %collective-permute-start) | collective-permute-done | bytes 4128 | tf_op jit(solution)/shard_map/ppermute | solution.py:509
  51.5 0.7 %add.9 = f32[8,128]{1,0:T(8,128)S(1)} add(f32[8,128]{1,0:T(8,128)} %get-tuple-element.20, f32[8,128]{1,0:T(8,128)S(1)} %collective-permute-done) | non-fusion elementwise | flops 1024 | bytes 12288 | tf_op jit(solution)/shard_map/add | solution.py:509
  52.2 1.6 %collective-permute-start.1 = (f32[8,128]{1,0:T(8,128)S(1)}, f32[8,128]{1,0:T(8,128)S(1)}, u32[]{:S(2)}, u32[]{:S(2)}) collective-permute-start(f32[8,128]{1,0:T(8,128)S(1)} %add.9), channel_id=1, source_target_pairs={{0,32},{64,96},{32,0},{96,64},{1,33},{65,97},{33,1},{97,65},{2,34}... | collective-permute-start | bytes 12296 | tf_op jit(solution)/shard_map/ppermute | solution.py:509
  53.8 2.0 %collective-permute-done.1 = f32[8,128]{1,0:T(8,128)S(1)} collective-permute-done((f32[8,128]{1,0:T(8,128)S(1)}, f32[8,128]{1,0:T(8,128)S(1)}, u32[]{:S(2)}, u32[]{:S(2)}) %collective-permute-start.1) | collective-permute-done | bytes 4128 | tf_op jit(solution)/shard_map/ppermute | solution.py:509
  55.8 3.0 %collective-permute-start.2 = (f32[8,128]{1,0:T(8,128)S(1)}, f32[8,128]{1,0:T(8,128)S(1)}, u32[]{:S(2)}, u32[]{:S(2)}) collective-permute-start(f32[8,128]{1,0:T(8,128)S(1)} %add.10), channel_id=1, source_target_pairs={{0,96},{32,64},{96,0},{64,32},{1,97},{33,65},{97,1},{65,33},{2,98}... | collective-permute-start | bytes 12296 | tf_op jit(solution)/shard_map/ppermute | solution.py:509
  58.8 1.8 %collective-permute-done.2 = f32[8,128]{1,0:T(8,128)S(1)} collective-permute-done((f32[8,128]{1,0:T(8,128)S(1)}, f32[8,128]{1,0:T(8,128)S(1)}, u32[]{:S(2)}, u32[]{:S(2)}) %collective-permute-start.2) | collective-permute-done | bytes 4128 | tf_op jit(solution)/shard_map/ppermute | solution.py:509
  60.7 0.5 multiply_bitcast_fusion
  (2 shorter events, 0.0 us)
Async XLA Ops:
  2.5 8.1 %copy-start.1 = (s32[3,1]{0,1:T(1,128)S(1)}, s32[3,1]{0,1:T(1,128)}, u32[]{:S(2)}) copy-start(s32[3,1]{0,1:T(1,128)} %param.13) | copy-start | bytes 40
  2.5 21.1 %all-to-all-start = ((f32[16,80,128]{2,1,0:T(8,128)}), f32[16,80,128]{2,1,0:T(8,128)S(1)}, u32[]{:S(2)}, u32[]{:S(2)}) async-start(f32[16,80,128]{2,1,0:T(8,128)} %bitcast.9), calls=%async_computation | async-start | bytes 1310720 | tf_op jit(solution)/shard_map/all_to_all | solution.py:521
  10.7 0.7 %copy-start.2 = (s32[3,1]{0,1:T(1,128)S(1)}, s32[3,1]{0,1:T(1,128)}, u32[]{:S(2)}) copy-start(s32[3,1]{0,1:T(1,128)} %param.15) | copy-start | bytes 40
  23.6 0.8 %copy-start = (f32[16,80,128]{2,1,0:T(8,128)}, f32[16,80,128]{2,1,0:T(8,128)S(1)}, u32[]{:S(2)}) copy-start(f32[16,80,128]{2,1,0:T(8,128)S(1)} %all-to-all-done) | copy-start | bytes 1966084
  50.2 1.4 %collective-permute-start = (f32[8,128]{1,0:T(8,128)}, f32[8,128]{1,0:T(8,128)S(1)}, u32[]{:S(2)}, u32[]{:S(2)}) collective-permute-start(f32[8,128]{1,0:T(8,128)} %get-tuple-element.20), channel_id=1, source_target_pairs={{0,16},{16,0},{1,17},{17,1},{2,18},{18,2},{3,19},{19,3},{4,20},{20... | collective-permute-start | bytes 12296 | tf_op jit(solution)/shard_map/ppermute | solution.py:509
  52.2 3.6 %collective-permute-start.1 = (f32[8,128]{1,0:T(8,128)S(1)}, f32[8,128]{1,0:T(8,128)S(1)}, u32[]{:S(2)}, u32[]{:S(2)}) collective-permute-start(f32[8,128]{1,0:T(8,128)S(1)} %add.9), channel_id=1, source_target_pairs={{0,32},{64,96},{32,0},{96,64},{1,33},{65,97},{33,1},{97,65},{2,34}... | collective-permute-start | bytes 12296 | tf_op jit(solution)/shard_map/ppermute | solution.py:509
  55.8 4.8 %collective-permute-start.2 = (f32[8,128]{1,0:T(8,128)S(1)}, f32[8,128]{1,0:T(8,128)S(1)}, u32[]{:S(2)}, u32[]{:S(2)}) collective-permute-start(f32[8,128]{1,0:T(8,128)S(1)} %add.10), channel_id=1, source_target_pairs={{0,96},{32,64},{96,0},{64,32},{1,97},{33,65},{97,1},{65,33},{2,98}... | collective-permute-start | bytes 12296 | tf_op jit(solution)/shard_map/ppermute | solution.py:509
where the time goes:
time: 61.6 us; the launch traced here: 61.2 us
  waiting for transfers between devices  16.8 us (27%)
  blocking collectives  16.8 us (27%)
  starting transfers between devices  12.7 us (21%)
  Pallas kernels  10.8 us (18%)
  local copies, waits for them, and re-layouts  2.18 us (4%)
  other arithmetic  1.2 us (2%)
  between operations  0.67 us (1%)
    all_to_all x1, blocking collectives, shards(): lax.all_to_all(back.reshape(OWNERS, BACK, 128), TILE, split_axis=0, conca...  16.8 us
    all_to_all x1, waiting for transfers between devices, shards(): lax.all_to_all(sent.reshape(OWNERS, SEND, 128), TILE, split_axis=0, conca...  11.6 us
    all_to_all x1, starting transfers between devices, shards(): lax.all_to_all(sent.reshape(OWNERS, SEND, 128), TILE, split_axis=0, conca...  8.12 us
    pallas_call x1, Pallas kernels, shards(): pl.pallas_call(render_kernel, out_shape=(shape(VIEWS, 3, 1, 256), shape(O...  6.75 us
    ppermute x3, waiting for transfers between devices, over_pairs(): return value + lax.ppermute(value, axis, both)  5.21 us
    ppermute x3, starting transfers between devices, over_pairs(): return value + lax.ppermute(value, axis, both)  4.59 us
    unnamed x8, local copies, waits for them, and re-layouts  2.18 us
    pallas_call x1, Pallas kernels, shards(): pl.pallas_call(adam_kernel, out_shape=(shape(59, 512), shape(59, 512), sh...  2.12 us
  transfers between devices with their start and end apart: 4, of which 4 were waited for; matrix products, arithmetic and copies ran while one was open for 2% of the time, Pallas kernels for 0%

commit v1 on v0

--- a/solution.py
+++ b/solution.py
@@ -9,6 +9,7 @@
 VIEWS = 3
 TILES_WIDE = 4
 TILE = ("tile_0", "tile_1")
+GAUSS = ("gauss_0", "gauss_1")
 GAUSS_TILE = ("gauss_0", "gauss_1", "tile_0", "tile_1")
 OWNERS = 16
 OWN = 512
@@ -17,6 +18,7 @@
 SEND = 4 * ROWS
 BACK = SEND + 8
 GROUPS = 6
+KEPT = 33
 LOG2E = 1.4426950408889634
 
 band_zero = 0.28209479177387814
@@ -118,7 +120,12 @@
     return lax.dot_general(lhs, rhs, (((0,), (0,)), ((), ())), preferred_element_type=f32)
 
 
-def render_kernel(
+def per_view(values):
+    place = iota((GROUPS, 128), 0)
+    return jnp.where(place < 2, values[0], jnp.where(place < 4, values[1], values[2]))
+
+
+def front_kernel(
     table_ref,
     lists_ref,
     counts_ref,
@@ -126,23 +133,20 @@
     camera_ref,
     target_ref,
     rendered_ref,
-    back_ref,
+    loss_ref,
+    shade_ref,
+    keep_ref,
+    pulled_ref,
+    stacked_ref,
+    tint_ref,
+    entry_ref,
     found_ref,
-    lane_ref,
     rows_ref,
     colour_ref,
-    shade_ref,
     logs_ref,
-    keep_ref,
     high_ref,
     low_ref,
-    moment_ref,
-    tint_ref,
-    grads_ref,
-    spread_ref,
-    places_ref,
     tri_ref,
-    loss_ref,
 ):
     quarter = iota((8, 128), 0) & 3
     for group in range(GROUPS):
@@ -176,10 +180,6 @@
             colour_ref[pl.ds(8 * view + k, 1), pl.ds(128 * half, 128)] = value
 
     place = iota((GROUPS, 128), 0)
-
-    def per_view(values):
-        return jnp.where(place < 2, values[0], jnp.where(place < 4, values[1], values[2]))
-
     camera = [per_view([camera_ref[view, i] for view in range(VIEWS)]) for i in range(8)]
     affine = (camera[0:3], camera[3:6])
     centre = [entry_row(i) for i in range(3)]
@@ -216,19 +216,23 @@
     middle_y = (tile // TILES_WIDE * 16 + 8).astype(f32)
     shift_x = mean[0] - middle_x
     shift_y = mean[1] - middle_y
-    quantities = [
-        shift_x,
-        shift_y,
-        (-0.5 * LOG2E) * conic[0],
-        (-LOG2E) * conic[1],
-        (-0.5 * LOG2E) * conic[2],
-        shown,
-    ]
-    for n, value in enumerate(quantities):
-        lane_ref[pl.ds(8 * n, GROUPS), :] = value
-    for n in range(len(quantities)):
+    kept = (
+        [shift_x, shift_y]
+        + [(-0.5 * LOG2E) * conic[0], (-LOG2E) * conic[1], (-0.5 * LOG2E) * conic[2]]
+        + [shown, opacity, inverse_norm, qw, qx, qy, qz]
+        + conic
+        + scale
+        + screen[0]
+        + screen[1]
+        + stretched[0]
+        + stretched[1]
+        + stretched[2]
+    )
+    for n, value in enumerate(kept):
+        entry_ref[pl.ds(8 * n, GROUPS), :] = value
+    for n in range(6):
         for half in range(2):
-            rows_ref[pl.ds(8 * n, VIEWS), pl.ds(128 * half, 128)] = lane_ref[
+            rows_ref[pl.ds(8 * n, VIEWS), pl.ds(128 * half, 128)] = entry_ref[
                 pl.ds(8 * n + half, VIEWS, stride=2), :
             ]
 
@@ -237,21 +241,8 @@
     strictly = jnp.where(before < after, 1.0, 0.0).astype(bf16)
     tri_ref[0:256, :] = strictly
     tri_ref[256:512, :] = strictly
-    strictly = jnp.where(before > after, 1.0, 0.0).astype(bf16)
-    tri_ref[512:768, :] = strictly
-    tri_ref[768:1024, :] = strictly
-    pixel = iota((16, 256), 1)
-    power = iota((16, 256), 0)
-    pixel_u = (pixel % 16).astype(f32) - 7.5
-    pixel_v = (pixel // 16).astype(f32) - 7.5
-    basis = jnp.where(power == 0, 1.0, jnp.where(power == 1, pixel_u, pixel_v))
-    basis = jnp.where(power == 3, pixel_u * pixel_u, basis)
-    basis = jnp.where(power == 4, pixel_u * pixel_v, basis)
-    basis = jnp.where(power == 5, pixel_v * pixel_v, basis)
-    basis = jnp.where(power > 5, 0.0, basis).astype(bf16)
     offset = iota((16, 256), 0).astype(f32) - 7.5
     loss_ref[...] = jnp.zeros_like(loss_ref)
-    kinds = iota((16, 256), 0)
 
     def one_view(view, carry):
         def row(n):
@@ -263,19 +254,21 @@
         along = row(2) * dx * dx
         across = row(3) * dx
         upright = row(4)
+        base = pl.multiple_of(256 * view, 256)
         for line in range(16):
             dy = (line - 7.5) - mean_v
             exponent = along + (upright * dy * dy + across * dy)
             shade = opaque * jnp.exp2(exponent)
-            shade_ref[pl.ds(16 * line, 16), :] = shade
+            shade_ref[pl.ds(base + 16 * line, 16), :] = shade
             high, low = split(jnp.log(1.0 - jnp.minimum(shade, 0.99)))
             logs_ref[pl.ds(16 * line, 16), 0:256] = high
             logs_ref[pl.ds(16 * line, 16), 256:512] = low
         for part in range(4):
             rows = pl.ds(64 * part, 64)
-            keep = jnp.exp(nn(logs_ref[rows, :], tri_ref[0:512, :]))
-            keep_ref[rows, :] = keep
-            high, low = split(jnp.minimum(shade_ref[rows, :], 0.99) * keep)
+            there = pl.ds(base + 64 * part, 64)
+            keep = jnp.exp(nn(logs_ref[rows, :], tri_ref[...]))
+            keep_ref[there, :] = keep
+            high, low = split(jnp.minimum(shade_ref[there, :], 0.99) * keep)
             high_ref[rows, :] = high
             low_ref[rows, :] = low
         colour = colour_ref[pl.ds(pl.multiple_of(8 * view, 8), 8), :]
@@ -312,19 +305,60 @@
         tint_ref[pl.ds(pl.multiple_of(8 * view, 8), 3), :] = (
             tint[0:3] + tint[3:6] + tint_low[0:3]
         )
-        pull = tn(pulled, stacked)
+        pulled_ref[pl.ds(pl.multiple_of(16 * view, 16), 16), :] = pulled
+        stacked_ref[pl.ds(pl.multiple_of(16 * view, 16), 16), :] = stacked
+        return carry
+
+    lax.fori_loop(0, VIEWS, one_view, 0)
+
+
+def back_kernel(
+    shade_ref,
+    keep_ref,
+    pulled_ref,
+    stacked_ref,
+    entry_ref,
+    camera_ref,
+    grads_ref,
+    logs_ref,
+    high_ref,
+    low_ref,
+    moment_ref,
+    tri_ref,
+):
+    before = iota((256, 256), 0)
+    after = iota((256, 256), 1)
+    strictly = jnp.where(before > after, 1.0, 0.0).astype(bf16)
+    tri_ref[0:256, :] = strictly
+    tri_ref[256:512, :] = strictly
+    pixel = iota((16, 256), 1)
+    power = iota((16, 256), 0)
+    pixel_u = (pixel % 16).astype(f32) - 7.5
+    pixel_v = (pixel // 16).astype(f32) - 7.5
+    basis = jnp.where(power == 0, 1.0, jnp.where(power == 1, pixel_u, pixel_v))
+    basis = jnp.where(power == 3, pixel_u * pixel_u, basis)
+    basis = jnp.where(power == 4, pixel_u * pixel_v, basis)
+    basis = jnp.where(power == 5, pixel_v * pixel_v, basis)
+    basis = jnp.where(power > 5, 0.0, basis).astype(bf16)
+
+    def one_view(view, carry):
+        base = pl.multiple_of(256 * view, 256)
+        small = pl.ds(pl.multiple_of(16 * view, 16), 16)
+        pull = tn(pulled_ref[small, :], stacked_ref[small, :])
         for part in range(4):
             rows = pl.ds(64 * part, 64)
-            weight = jnp.minimum(shade_ref[rows, :], 0.99) * keep_ref[rows, :]
+            there = pl.ds(base + 64 * part, 64)
+            weight = jnp.minimum(shade_ref[there, :], 0.99) * keep_ref[there, :]
             high, low = split(pull[64 * part : 64 * part + 64] * weight)
             logs_ref[rows, 0:256] = high
             logs_ref[rows, 256:512] = low
         for part in range(4):
             rows = pl.ds(64 * part, 64)
-            behind = nn(logs_ref[rows, :], tri_ref[512:1024, :])
-            shade = shade_ref[rows, :]
+            there = pl.ds(base + 64 * part, 64)
+            behind = nn(logs_ref[rows, :], tri_ref[...])
+            shade = shade_ref[there, :]
             alpha = jnp.minimum(shade, 0.99)
-            slope = pull[64 * part : 64 * part + 64] * keep_ref[rows, :] - behind / (1.0 - alpha)
+            slope = pull[64 * part : 64 * part + 64] * keep_ref[there, :] - behind / (1.0 - alpha)
             passed = jnp.where(shade < 0.99, shade, jnp.where(shade == 0.99, 0.5 * shade, 0.0))
             high, low = split(slope * passed)
             high_ref[rows, :] = high
@@ -338,6 +372,15 @@
 
     lax.fori_loop(0, VIEWS, one_view, 0)
 
+    kept = [entry_ref[pl.ds(8 * n, GROUPS), :] for n in range(KEPT)]
+    shift_x, shift_y = kept[0:2]
+    opacity, inverse_norm, qw, qx, qy, qz = kept[6:12]
+    conic = kept[12:15]
+    scale = kept[15:18]
+    screen = (kept[18:21], kept[21:24])
+    stretched = (kept[24:27], kept[27:30], kept[30:33])
+    camera = [per_view([camera_ref[view, i] for view in range(VIEWS)]) for i in range(6)]
+    affine = (camera[0:3], camera[3:6])
     m_0, m_u, m_v, m_uu, m_uv, m_vv = [
         moment_ref[pl.ds(8 * n, GROUPS), :] for n in range(6)
     ]
@@ -401,6 +444,19 @@
         grads_ref[pl.ds(16 * n, GROUPS), :] = high
         grads_ref[pl.ds(16 * n + 8, GROUPS), :] = value - high
 
+
+def scatter_kernel(
+    lists_ref,
+    grads_ref,
+    tint_ref,
+    loss_ref,
+    core_ref,
+    side_ref,
+    across_ref,
+    back_ref,
+    spread_ref,
+    places_ref,
+):
     coarse = iota((32, 128), 0)
     fine = iota((256, 128), 0)
     kinds_of = GEOMETRY * 32
@@ -425,6 +481,8 @@
                     chosen * jnp.broadcast_to(piece, (32, 128)).astype(bf16)
                 )
 
+    losses = (loss_ref[...] + core_ref[...]) + (side_ref[...] + across_ref[...])
+
     def store(row, value):
         for upper in range(2):
             for side in range(2):
@@ -444,11 +502,19 @@
                 dense[32 * k : 32 * k + 32] + dense[96 + 32 * k : 96 + 32 * k + 32],
             )
     for owner in range(OWNERS):
-        back_ref[pl.ds(BACK * owner + SEND, 8), :] = loss_ref[...]
+        back_ref[pl.ds(BACK * owner + SEND, 8), :] = losses
+
+
+def fold_kernel(back_ref, total_ref, loss_ref):
+    total = back_ref[0:BACK, :]
+    for owner in range(1, OWNERS):
+        total = total + back_ref[pl.ds(BACK * owner, BACK), :]
+    total_ref[...] = total[0:SEND]
+    loss_ref[...] = total[SEND:BACK]
 
 
 def adam_kernel(
-    back_ref,
+    total_ref,
     slope_ref,
     params_ref,
     moment_one_ref,
@@ -457,15 +523,8 @@
     params_out,
     first_out,
     second_out,
-    loss_out,
-    total_ref,
     gradient_ref,
 ):
-    total = back_ref[0:BACK, :]
-    for owner in range(1, OWNERS):
-        total = total + back_ref[pl.ds(BACK * owner, BACK), :]
-    total_ref[...] = total
-    loss_out[...] = total[SEND : SEND + 8]
     columns = [harmonic_halves(camera_ref, view) for view in range(VIEWS)]
     row = iota((59, 128), 0)
     rates = jnp.where(row < 14, 0.0025, 0.000125)
@@ -504,9 +563,12 @@
     return jax.ShapeDtypeStruct(dims, f32)
 
 
-def over_pairs(value, axis, pairs):
-    both = [(a, b) for a, b in pairs] + [(b, a) for a, b in pairs]
-    return value + lax.ppermute(value, axis, both)
+def swapped(value, partner):
+    return lax.ppermute(value, GAUSS, [(i, partner(i)) for i in range(8)])
+
+
+def limit(mib):
+    return pltpu.CompilerParams(vmem_limit_bytes=mib << 20)
 
 
 def shards(params, moment_one, moment_two, camera, target, tile_ids, splat_lists, counts):
@@ -521,46 +583,92 @@
     table = lax.all_to_all(
         sent.reshape(OWNERS, SEND, 128), TILE, split_axis=0, concat_axis=0, tiled=True
     ).reshape(OWNERS * SEND, 128)
-    rendered, back = pl.pallas_call(
-        render_kernel,
-        out_shape=(shape(VIEWS, 3, 1, 256), shape(OWNERS * BACK, 128)),
+    half = jax.ShapeDtypeStruct((48, 256), bf16)
+    rendered, loss, shade, keep, pulled, stacked, tint, entries = pl.pallas_call(
+        front_kernel,
+        out_shape=(
+            shape(VIEWS, 3, 1, 256),
+            shape(8, 128),
+            shape(VIEWS * 256, 256),
+            shape(VIEWS * 256, 256),
+            half,
+            half,
+            shape(24, 256),
+            shape(8 * KEPT, 128),
+        ),
         in_specs=[VM, VM, SM, SM, SM, VM],
-        out_specs=(VM, VM),
+        out_specs=(VM,) * 8,
         scratch_shapes=[
             pltpu.VMEM((GROUPS * SEND, 128), f32),
-            pltpu.VMEM((48, 128), f32),
             pltpu.VMEM((48, 256), f32),
             pltpu.VMEM((24, 256), f32),
-            pltpu.VMEM((256, 256), f32),
             pltpu.VMEM((256, 512), bf16),
-            pltpu.VMEM((256, 256), f32),
+            pltpu.VMEM((256, 256), bf16),
+            pltpu.VMEM((256, 256), bf16),
+            pltpu.VMEM((512, 256), bf16),
+        ],
+        compiler_params=limit(16),
+        name="front",
+    )(table, splat_lists, counts, tile_ids, camera, target)
+    core = swapped(loss, lambda i: i ^ 1)
+    side = swapped(loss, lambda i: i ^ 2)
+    across = swapped(loss, lambda i: i ^ 3)
+    grads = pl.pallas_call(
+        back_kernel,
+        out_shape=shape(16 * GEOMETRY, 128),
+        in_specs=[VM, VM, VM, VM, VM, SM],
+        out_specs=VM,
+        scratch_shapes=[
+            pltpu.VMEM((256, 512), bf16),
             pltpu.VMEM((256, 256), bf16),
             pltpu.VMEM((256, 256), bf16),
             pltpu.VMEM((64, 128), f32),
-            pltpu.VMEM((24, 256), f32),
-            pltpu.VMEM((16 * GEOMETRY, 128), f32),
+            pltpu.VMEM((512, 256), bf16),
+        ],
+        compiler_params=limit(12),
+        cost_estimate=pl.CostEstimate(
+            flops=1 << 31, bytes_accessed=1 << 23, transcendentals=1 << 20
+        ),
+        name="back",
+    )(shade, keep, pulled, stacked, entries, camera)
+    back = pl.pallas_call(
+        scatter_kernel,
+        out_shape=shape(OWNERS * BACK, 128),
+        in_specs=[VM] * 7,
+        out_specs=VM,
+        scratch_shapes=[
             pltpu.VMEM((2 * 32 * GEOMETRY + 192, 768), bf16),
             pltpu.VMEM((256, 768), bf16),
-            pltpu.VMEM((1024, 256), bf16),
-            pltpu.VMEM((8, 128), f32),
         ],
-        name="render",
-    )(table, splat_lists, counts, tile_ids, camera, target)
+        compiler_params=limit(12),
+        name="scatter",
+    )(splat_lists, grads, tint, loss, core, side, across)
     arrived = lax.all_to_all(
         back.reshape(OWNERS, BACK, 128), TILE, split_axis=0, concat_axis=0, tiled=True
     ).reshape(OWNERS * BACK, 128)
-    updated, first, second, loss = pl.pallas_call(
+    total, loss = pl.pallas_call(
+        fold_kernel,
+        out_shape=(shape(SEND, 128), shape(8, 128)),
+        in_specs=[VM],
+        out_specs=(VM, VM),
+        compiler_params=limit(4),
+        name="fold",
+    )(arrived)
+    other = swapped(loss, lambda i: 6 - (i & 6) + (i & 1))
+    updated, first, second = pl.pallas_call(
         adam_kernel,
-        out_shape=(shape(59, 512), shape(59, 512), shape(59, 512), shape(8, 128)),
+        out_shape=(shape(59, 512), shape(59, 512), shape(59, 512)),
         in_specs=[VM, VM, VM, VM, VM, SM],
-        out_specs=(VM, VM, VM, VM),
-        scratch_shapes=[pltpu.VMEM((BACK, 128), f32), pltpu.VMEM((256, 128), f32)],
+        out_specs=(VM, VM, VM),
+        scratch_shapes=[pltpu.VMEM((256, 128), f32)],
+        compiler_params=limit(4),
+        cost_estimate=pl.CostEstimate(
+            flops=1 << 30, bytes_accessed=1 << 22, transcendentals=1 << 16
+        ),
         name="adam",
-    )(arrived, slope, params, moment_one, moment_two, camera)
-    loss = over_pairs(loss, "gauss_1", [(0, 1)])
-    loss = over_pairs(loss, "gauss_0", [(0, 1), (2, 3)])
-    loss = over_pairs(loss, "gauss_0", [(0, 3), (1, 2)])
-    return (updated, first, second, rendered, loss[0, :VIEWS] * (0.5 / (3 * 256 * 128)))
+    )(total, slope, params, moment_one, moment_two, camera)
+    losses = (loss + other)[0, :VIEWS] * (0.5 / (3 * 256 * 128))
+    return (updated, first, second, rendered, losses)
 
 
 def solution(mesh):

time: 61.6 us -> 55.2 us (0.90)
  waiting for transfers between devices: 16.8 us -> 13.3 us
  local copies, waits for them, and re-layouts: 2.18 us -> 0.22 us
  other arithmetic: 1.2 us -> 0.52 us
    ppermute x3 -> x4, waiting for transfers between devices: 5.21 us -> 0.61 us  [swapped(): return lax.ppermute(value, GAUSS, [(i, partner(i)) for i in range(8)])]
    unnamed x8 -> x20, local copies, waits for them, and re-layouts: 2.18 us -> 0.22 us
    all_to_all x1, waiting for transfers between devices: 11.6 us -> 12.7 us  [shards(): lax.all_to_all(sent.reshape(OWNERS, SEND, 128), TILE, split_axis=0, conca...]
    pallas_call x1, Pallas kernels: 2.12 us -> 1.41 us  [shards(): pl.pallas_call(adam_kernel, out_shape=(shape(59, 512), shape(59, 512), sh...]
    add x3 -> x1, other arithmetic: 0.68 us -> 0.01 us  [shards(): losses = (loss + other)[0, :VIEWS] * (0.5 / (3 * 256 * 128))]
    pallas_call x1 -> x4, Pallas kernels: 6.75 us -> 6.9 us  [the longest x1 3.79 us: shards(): pl.pallas_call(front_kernel, out_shape=(shape(VIEWS, 3, 1, 256), shape(8,...]
    ppermute x3 -> x4, starting transfers between devices: 4.59 us -> 4.73 us  [swapped(): return lax.ppermute(value, GAUSS, [(i, partner(i)) for i in range(8)])]
  transfers between devices with their start and end apart: 4 -> 5, of which waited for: 4 -> 2; matrix products, arithmetic and copies ran while one was open for 2% -> 0% of each run, Pallas kernels for 0% -> 7%
where the time goes in v1:
time: 55.2 us; the launch traced here: 54.9 us
  blocking collectives  17 us (31%)
  waiting for transfers between devices  13.3 us (24%)
  starting transfers between devices  12.9 us (23%)
  Pallas kernels  10.2 us (18%)
  between operations  0.72 us (1%)
    all_to_all x1, blocking collectives, shards(): lax.all_to_all(back.reshape(OWNERS, BACK, 128), TILE, split_axis=0, conca...  17 us
    all_to_all x1, waiting for transfers between devices, shards(): lax.all_to_all(sent.reshape(OWNERS, SEND, 128), TILE, split_axis=0, conca...  12.7 us
    all_to_all x1, starting transfers between devices, shards(): lax.all_to_all(sent.reshape(OWNERS, SEND, 128), TILE, split_axis=0, conca...  8.13 us
    ppermute x4, starting transfers between devices, swapped(): return lax.ppermute(value, GAUSS, [(i, partner(i)) for i in range(8)])  4.73 us
    pallas_call x1, Pallas kernels, shards(): pl.pallas_call(front_kernel, out_shape=(shape(VIEWS, 3, 1, 256), shape(8,...  3.79 us
    pallas_call x1, Pallas kernels, shards(): pl.pallas_call(back_kernel, out_shape=shape(16 * GEOMETRY, 128), in_specs...  2.42 us
    pallas_call x1, Pallas kernels, shards(): pl.pallas_call(pack_kernel, out_shape=(shape(OWNERS * SEND, 128), shape(3...  1.88 us
    pallas_call x1, Pallas kernels, shards(): pl.pallas_call(adam_kernel, out_shape=(shape(59, 512), shape(59, 512), sh...  1.41 us
  transfers between devices with their start and end apart: 5, of which 2 were waited for; matrix products, arithmetic and copies ran while one was open for 0% of the time, Pallas kernels for 7%

profile of v1, /device:TPU:0, one launch (start us, length us, event | category | flops | bytes accessed | tf_op | source)
XLA Modules:
  0.0 54.9 jit_solution(1065058601906834152)
XLA Ops:
  0.6 1.9 %pack.1 = (f32[1280,128]{1,0:T(8,128)}, f32[36,128]{1,0:T(8,128)}) custom-call(f32[59,512]{1,0:T(8,128)} %params_ref.3, f32[3,11]{1,0:T(4,128)} %camera_ref.7), custom_call_target="tpu_custom_call" | custom-call | tf_op jit(solution)/shard_map/pack/pallas_call | solution.py:575
  2.5 8.1 %all-to-all-start = ((f32[16,80,128]{2,1,0:T(8,128)}), f32[16,80,128]{2,1,0:T(8,128)S(1)}, u32[]{:S(2)}, u32[]{:S(2)}) async-start(f32[16,80,128]{2,1,0:T(8,128)} %bitcast.9), calls=%async_computation | async-start | bytes 1310720 | tf_op jit(solution)/shard_map/all_to_all | solution.py:583
  10.7 0.0 copy-done.7
  10.7 0.0 copy-start.1
  10.7 0.1 copy.14.tiles_ref
  10.8 0.0 copy-done.8
  10.8 0.1 copy.13.counts_ref
  10.9 12.7 %all-to-all-done = f32[16,80,128]{2,1,0:T(8,128)S(1)} async-done(((f32[16,80,128]{2,1,0:T(8,128)}), f32[16,80,128]{2,1,0:T(8,128)S(1)}, u32[]{:S(2)}, u32[]{:S(2)}) %all-to-all-start) | async-done | bytes 655392 | tf_op jit(solution)/shard_map/all_to_all | solution.py:583
  23.6 0.0 copy-done.2
  23.6 0.0 copy-done.1
  23.6 3.8 %front.1 = (f32[3,3,1,256]{3,2,1,0:T(1,128)}, f32[8,128]{1,0:T(8,128)S(1)}, f32[768,256]{1,0:T(8,128)S(1)}, f32[768,256]{1,0:T(8,128)S(1)}, bf16[48,256]{1,0:T(8...) custom-call(f32[1280,128]{1,0:T(8,128)S(1)} %bitcast.8, ...), custom_call_target="tpu_custom_call" | custom-call | tf_op jit(solution)/shard_map/front/pallas_call | solution.py:587
  27.4 0.0 collective-permute-start.2
  27.4 1.6 %collective-permute-start.1 = (f32[8,128]{1,0:T(8,128)S(1)}, f32[8,128]{1,0:T(8,128)S(1)}, u32[]{:S(2)}, u32[]{:S(2)}) collective-permute-start(f32[8,128]{1,0:T(8,128)S(1)} %get-tuple-element.27.loss_ref), channel_id=1, source_target_pairs={{0,32},{16,48},{32,0},{48,16},{64,96},{80,112},{96,64},{112,80},{1... | collective-permute-start | bytes 12296 | tf_op jit(solution)/shard_map/ppermute | solution.py:567
  29.0 0.3 collective-permute-start
  29.3 2.4 %back.1.grads_ref = f32[176,128]{1,0:T(8,128)S(1)} custom-call(f32[768,256]{1,0:T(8,128)S(1)} %get-tuple-element.21.shade_ref, f32[768,256]{1,0:T(8,128)S(1)} %get-tuple-element.22.keep_ref, bf16[48,256]{1,0:T(8,128)(2,1)S(1)} %get-tuple-element.23.pulled_ref, bf16[48,256]{1,0:T(8,128)(2,1)S(1)} %get-tuple-element.24.stacked_ref, ...), custom_call_target="tpu_custom_call" | custom-call | flops 2147483648 | bytes 8388608 | tf_op jit(solution)/shard_map/back/pallas_call | solution.py:616
  31.7 0.0 collective-permute-done.2.across_ref
  31.7 0.0 collective-permute-done.1.side_ref
  31.7 0.0 collective-permute-done.core_ref
  31.7 0.6 %scatter.1 = f32[1408,128]{1,0:T(8,128)S(1)} custom-call(s32[3,1,256]{2,1,0:T(1,128)S(1)} %copy-done.1, f32[176,128]{1,0:T(8,128)S(1)} %back.1.grads_ref, f32[24,256]{1,0:T(8,128)S(1)} %get-tuple-element.26.tint_ref, f32[8,128]{1,0:T(8,128)S(1)} %get-tuple-element.27.loss_ref, f32[8,128]{1,0:T(8,128)S(1)} %collective-permute-done.core_ref, ...), custom_call_target="tpu_custom_call" | custom-call | tf_op jit(solution)/shard_map/scatter/pallas_call | solution.py:634
  32.4 17.0 %all_to_all.10 = f32[16,88,128]{2,1,0:T(8,128)S(1)} all-to-all(f32[16,88,128]{2,1,0:T(8,128)S(1)} %bitcast.6), channel_id=1, replica_groups=mesh['gauss_0'=4,'gauss_1'=2,'tile_0'=4,'tile_1'=4] {'tile_0','tile_1'}, dimensions={0} | all-to-all | bytes 1441792 | tf_op jit(solution)/shard_map/all_to_all | solution.py:646
  49.5 2.9 %collective-permute-start.3 = (f32[8,128]{1,0:T(8,128)S(1)}, f32[8,128]{1,0:T(8,128)S(1)}, u32[]{:S(2)}, u32[]{:S(2)}) collective-permute-start(f32[8,128]{1,0:T(8,128)S(1)} %get-tuple-element.34), channel_id=1, source_target_pairs={{0,96},{16,112},{32,64},{48,80},{64,32},{80,48},{96,0},{112,16},{1... | collective-permute-start | bytes 12296 | tf_op jit(solution)/shard_map/ppermute | solution.py:567
  52.3 1.4 %adam.1 = (f32[59,512]{1,0:T(8,128)}, f32[59,512]{1,0:T(8,128)}, f32[59,512]{1,0:T(8,128)}) custom-call(f32[80,128]{1,0:T(8,128)S(1)} %get-tuple-element.28.total_ref, f32[36,128]{1,0:T(8,128)S(1)} %copy-done.6, f32[59,512]{1,0:T(8,128)S(1)} %copy-done, f32[59,512]{1,0:T(8,128)S(1)} %copy-done.4, f32[59,512]{1,0:T(8,128)S(1)} %copy-done.5, f32[3,11]{1,0:T(4,128)S(1)} %copy-done.3), custom_call_target="tpu_custom_call" | custom-call | flops 1073741824 | bytes 4194304 | tf_op jit(solution)/shard_map/adam/pallas_call | solution.py:658
  53.8 0.6 %collective-permute-done.3 = f32[8,128]{1,0:T(8,128)S(1)} collective-permute-done((f32[8,128]{1,0:T(8,128)S(1)}, f32[8,128]{1,0:T(8,128)S(1)}, u32[]{:S(2)}, u32[]{:S(2)}) %collective-permute-start.3) | collective-permute-done | bytes 4128 | tf_op jit(solution)/shard_map/ppermute | solution.py:567
  54.4 0.5 multiply_bitcast_fusion
  (15 shorter events, 0.1 us)
Async XLA Ops:
  2.5 8.2 %copy-start.7 = (s32[3,1]{0,1:T(1,128)S(1)}, s32[3,1]{0,1:T(1,128)}, u32[]{:S(2)}) copy-start(s32[3,1]{0,1:T(1,128)} %param.13) | copy-start | bytes 40
  2.5 8.3 %copy-start.8 = (s32[3,1]{0,1:T(1,128)S(1)}, s32[3,1]{0,1:T(1,128)}, u32[]{:S(2)}) copy-start(s32[3,1]{0,1:T(1,128)} %param.15) | copy-start | bytes 40
  2.5 21.1 %copy-start.2 = (f32[3,3,1,256]{3,2,1,0:T(1,128)S(1)}, f32[3,3,1,256]{3,2,1,0:T(1,128)}, u32[]{:S(2)}) copy-start(f32[3,3,1,256]{3,2,1,0:T(1,128)} %target_ref.1) | copy-start | bytes 27652
  2.5 21.1 %all-to-all-start = ((f32[16,80,128]{2,1,0:T(8,128)}), f32[16,80,128]{2,1,0:T(8,128)S(1)}, u32[]{:S(2)}, u32[]{:S(2)}) async-start(f32[16,80,128]{2,1,0:T(8,128)} %bitcast.9), calls=%async_computation | async-start | bytes 1310720 | tf_op jit(solution)/shard_map/all_to_all | solution.py:583
  10.7 12.9 %copy-start.1 = (s32[3,1,256]{2,1,0:T(1,128)S(1)}, s32[3,1,256]{2,1,0:T(1,128)}, u32[]{:S(2)}) copy-start(s32[3,1,256]{2,1,0:T(1,128)} %lists_ref.3) | copy-start | bytes 9220
  10.8 12.8 %copy-start.3 = (f32[3,11]{1,0:T(4,128)S(1)}, f32[3,11]{1,0:T(4,128)}, u32[]{:S(2)}) copy-start(f32[3,11]{1,0:T(4,128)} %camera_ref.7) | copy-start | bytes 400
  27.4 4.3 %collective-permute-start.2 = (f32[8,128]{1,0:T(8,128)S(1)}, f32[8,128]{1,0:T(8,128)S(1)}, u32[]{:S(2)}, u32[]{:S(2)}) collective-permute-start(f32[8,128]{1,0:T(8,128)S(1)} %get-tuple-element.27.loss_ref), channel_id=1, source_target_pairs={{0,48},{16,32},{32,16},{48,0},{64,112},{80,96},{96,80},{112,64},{1... | collective-permute-start | bytes 12296 | tf_op jit(solution)/shard_map/ppermute | solution.py:567
  27.4 4.3 %collective-permute-start.1 = (f32[8,128]{1,0:T(8,128)S(1)}, f32[8,128]{1,0:T(8,128)S(1)}, u32[]{:S(2)}, u32[]{:S(2)}) collective-permute-start(f32[8,128]{1,0:T(8,128)S(1)} %get-tuple-element.27.loss_ref), channel_id=1, source_target_pairs={{0,32},{16,48},{32,0},{48,16},{64,96},{80,112},{96,64},{112,80},{1... | collective-permute-start | bytes 12296 | tf_op jit(solution)/shard_map/ppermute | solution.py:567
  29.0 2.7 %collective-permute-start = (f32[8,128]{1,0:T(8,128)S(1)}, f32[8,128]{1,0:T(8,128)S(1)}, u32[]{:S(2)}, u32[]{:S(2)}) collective-permute-start(f32[8,128]{1,0:T(8,128)S(1)} %get-tuple-element.27.loss_ref), channel_id=1, source_target_pairs={{0,16},{16,0},{32,48},{48,32},{64,80},{80,64},{96,112},{112,96},{1... | collective-permute-start | bytes 12296 | tf_op jit(solution)/shard_map/ppermute | solution.py:567
  49.4 2.9 %copy-start = (f32[59,512]{1,0:T(8,128)S(1)}, f32[59,512]{1,0:T(8,128)}, u32[]{:S(2)}) copy-start(f32[59,512]{1,0:T(8,128)} %params_ref.3) | copy-start | bytes 362500
  49.4 2.9 %copy-start.4 = (f32[59,512]{1,0:T(8,128)S(1)}, f32[59,512]{1,0:T(8,128)}, u32[]{:S(2)}) copy-start(f32[59,512]{1,0:T(8,128)} %moment_one_ref.1) | copy-start | bytes 362500
  49.4 2.9 %copy-start.5 = (f32[59,512]{1,0:T(8,128)S(1)}, f32[59,512]{1,0:T(8,128)}, u32[]{:S(2)}) copy-start(f32[59,512]{1,0:T(8,128)} %moment_two_ref.1) | copy-start | bytes 362500
  49.4 2.9 %copy-start.6 = (f32[36,128]{1,0:T(8,128)S(1)}, f32[36,128]{1,0:T(8,128)}, u32[]{:S(2)}) copy-start(f32[36,128]{1,0:T(8,128)} %get-tuple-element.29.slope_ref) | copy-start | bytes 55300
  49.5 4.9 %collective-permute-start.3 = (f32[8,128]{1,0:T(8,128)S(1)}, f32[8,128]{1,0:T(8,128)S(1)}, u32[]{:S(2)}, u32[]{:S(2)}) collective-permute-start(f32[8,128]{1,0:T(8,128)S(1)} %get-tuple-element.34), channel_id=1, source_target_pairs={{0,96},{16,112},{32,64},{48,80},{64,32},{80,48},{96,0},{112,16},{1... | collective-permute-start | bytes 12296 | tf_op jit(solution)/shard_map/ppermute | solution.py:567

commit v2 on v1

--- a/solution.py
+++ b/solution.py
@@ -13,12 +13,12 @@
 GAUSS_TILE = ("gauss_0", "gauss_1", "tile_0", "tile_1")
 OWNERS = 16
 OWN = 512
-GEOMETRY = 11
-ROWS = 20
-SEND = 4 * ROWS
-BACK = SEND + 8
+GEOMETRY = 10
+COLOURS = 4 * GEOMETRY
+ERRORS = COLOURS + 36
+SEND = ERRORS + 4
 GROUPS = 6
-KEPT = 33
+KEPT = 32
 LOG2E = 1.4426950408889634
 
 band_zero = 0.28209479177387814
@@ -79,13 +79,31 @@
     return halves
 
 
-def pack_kernel(params_ref, camera_ref, send_ref, slope_ref, pack_ref, tall_ref):
+def per_view(values):
+    place = iota((GROUPS, 128), 0)
+    return jnp.where(place < 2, values[0], jnp.where(place < 4, values[1], values[2]))
+
+
+def pack_kernel(
+    params_hbm, camera_hbm, send_ref, slope_ref, params_ref, pack_ref, tall_ref, camera_ref, sems
+):
+    copies = [
+        pltpu.make_async_copy(camera_hbm, camera_ref, sems.at[0]),
+        pltpu.make_async_copy(params_hbm, params_ref, sems.at[1]),
+    ]
+    for copy in copies:
+        copy.start()
+    copies[0].wait()
+    columns = [harmonic_halves(camera_ref, view) for view in range(VIEWS)]
+    copies[1].wait()
     for quarter in range(4):
         lanes = pl.ds(128 * quarter, 128)
-        pack_ref[pl.ds(quarter, 8, stride=4), :] = params_ref[0:8, lanes]
-        pack_ref[pl.ds(32 + quarter, 3, stride=4), :] = params_ref[8:11, lanes]
+        pack_ref[pl.ds(quarter, 6, stride=4), :] = params_ref[0:6, lanes]
+        pack_ref[pl.ds(24 + quarter, 3, stride=4), :] = (
+            params_ref[7:10, lanes] / params_ref[6:7, lanes]
+        )
+        pack_ref[pl.ds(36 + quarter, 1), :] = params_ref[10:11, lanes]
         tall_ref[pl.ds(64 * quarter, 59), :] = params_ref[:, lanes]
-    columns = [harmonic_halves(camera_ref, view) for view in range(VIEWS)]
     for k in range(3):
         for quarter in range(4):
             low = tall_ref[pl.ds(64 * quarter + 11 + k, 8, stride=3), :]
@@ -94,45 +112,100 @@
                 terms = columns[view][0] * low + columns[view][1] * high
                 raw = jnp.sum(terms, axis=0, keepdims=True) + 0.5
                 row = 4 * (3 * view + k) + quarter
-                pack_ref[pl.ds(4 * GEOMETRY + row, 1), :] = jnp.maximum(raw, 0.0)
+                pack_ref[pl.ds(COLOURS + row, 1), :] = jnp.maximum(raw, 0.0)
                 slope_ref[pl.ds(row, 1), :] = jnp.where(
                     raw > 0.0, 1.0, jnp.where(raw == 0.0, 0.5, 0.0)
                 )
+    pack_ref[pl.ds(ERRORS, 4), :] = jnp.zeros((4, 128), f32)
     packed = pack_ref[...]
     for owner in range(OWNERS):
         send_ref[pl.ds(SEND * owner, SEND), :] = packed
 
 
-def split(value):
-    high = value.astype(bf16)
-    return high, (value - high.astype(f32)).astype(bf16)
-
-
-def nn(lhs, rhs):
-    return lax.dot_general(lhs, rhs, (((1,), (0,)), ((), ())), preferred_element_type=f32)
-
-
-def nt(lhs, rhs):
-    return lax.dot_general(lhs, rhs, (((1,), (1,)), ((), ())), preferred_element_type=f32)
-
-
-def tn(lhs, rhs):
-    return lax.dot_general(lhs, rhs, (((0,), (0,)), ((), ())), preferred_element_type=f32)
-
-
-def per_view(values):
-    place = iota((GROUPS, 128), 0)
-    return jnp.where(place < 2, values[0], jnp.where(place < 4, values[1], values[2]))
-
-
-def front_kernel(
-    table_ref,
+def prepare_kernel(
     lists_ref,
     counts_ref,
     tiles_ref,
     camera_ref,
+    lane_ref,
+    block_ref,
+    cast_ref,
+    column_ref,
+    places_ref,
+    chosen_ref,
+    before_ref,
+    behind_ref,
+    basis_ref,
+):
+    quarter = iota((8, 128), 0) & 3
+    fine = iota((256, 128), 0)
+    coarse = iota((32, 128), 0)
+    for group in range(GROUPS):
+        view, half = divmod(group, 2)
+        local = lists_ref[view, :, 128 * half : 128 * half + 128] & 8191
+        spread = jnp.broadcast_to(local, (8, 128))
+        lane_ref[pl.ds(8 * group, 8), :] = spread & 127
+        block_ref[pl.ds(8 * group, 8), :] = (spread >> 7) - quarter
+        lanes = pl.ds(128 * group, 128)
+        places_ref[:, lanes] = jnp.where((local & 255) == fine, 1.0, 0.0).astype(bf16)
+        owner_part = ((local >> 8) & 1) * 16 + (local >> 9)
+        chosen_ref[:, lanes] = jnp.where(owner_part == coarse, 1.0, 0.0).astype(bf16)
+    for i in range(8):
+        cast_ref[pl.ds(8 * i, GROUPS), :] = per_view(
+            [camera_ref[view, i] for view in range(VIEWS)]
+        )
+    place = iota((GROUPS, 128), 0)
+    position = (place & 1) * 128 + iota((GROUPS, 128), 1)
+    live = position < per_view([counts_ref[view, 0] for view in range(VIEWS)])
+    cast_ref[pl.ds(64, GROUPS), :] = jnp.where(live, 1.0, 0.0)
+    tile = per_view([tiles_ref[view, 0] for view in range(VIEWS)])
+    cast_ref[pl.ds(72, GROUPS), :] = (tile % TILES_WIDE * 16 + 8).astype(f32)
+    cast_ref[pl.ds(80, GROUPS), :] = (tile // TILES_WIDE * 16 + 8).astype(f32)
+    for view in range(VIEWS):
+        for half, column in enumerate(harmonic_halves(camera_ref, view)):
+            column_ref[pl.ds(16 * view + 8 * half, 8), :] = column
+    first = iota((256, 256), 0)
+    second = iota((256, 256), 1)
+    for ref, strictly in ((before_ref, first < second), (behind_ref, first > second)):
+        ones = jnp.where(strictly, 1.0, 0.0).astype(bf16)
+        ref[0:256, :] = ones
+        ref[256:512, :] = ones
+    pixel = iota((16, 256), 1)
+    power = iota((16, 256), 0)
+    pixel_u = (pixel % 16).astype(f32) - 7.5
+    pixel_v = (pixel // 16).astype(f32) - 7.5
+    basis = jnp.where(power == 0, 1.0, jnp.where(power == 1, pixel_u, pixel_v))
+    basis = jnp.where(power == 3, pixel_u * pixel_u, basis)
+    basis = jnp.where(power == 4, pixel_u * pixel_v, basis)
+    basis = jnp.where(power == 5, pixel_v * pixel_v, basis)
+    basis_ref[...] = jnp.where(power > 5, 0.0, basis).astype(bf16)
+
+
+def split(value):
+    high = value.astype(bf16)
+    return high, (value - high.astype(f32)).astype(bf16)
+
+
+def nn(lhs, rhs):
+    return lax.dot_general(lhs, rhs, (((1,), (0,)), ((), ())), preferred_element_type=f32)
+
+
+def nt(lhs, rhs):
+    return lax.dot_general(lhs, rhs, (((1,), (1,)), ((), ())), preferred_element_type=f32)
+
+
+def tn(lhs, rhs):
+    return lax.dot_general(lhs, rhs, (((0,), (0,)), ((), ())), preferred_element_type=f32)
+
+
+def front_kernel(
+    table_ref,
+    lane_ref,
+    block_ref,
+    cast_ref,
+    before_ref,
     target_ref,
-    rendered_ref,
+    image_ref,
     loss_ref,
     shade_ref,
     keep_ref,
@@ -146,18 +219,14 @@
     logs_ref,
     high_ref,
     low_ref,
-    tri_ref,
 ):
-    quarter = iota((8, 128), 0) & 3
     for group in range(GROUPS):
         view, half = divmod(group, 2)
-        local = lists_ref[view, :, 128 * half : 128 * half + 128] & 8191
-        local = jnp.broadcast_to(local, (8, 128))
-        lane = local & 127
-        block = (local >> 7) - quarter
-        first = (4 * (GEOMETRY + 3 * view)) // 8
-        last = (4 * (GEOMETRY + 3 * view + 3) - 1) // 8
-        pieces = sorted(set(range(6)) | set(range(first, last + 1)))
+        lane = lane_ref[pl.ds(8 * group, 8), :]
+        block = block_ref[pl.ds(8 * group, 8), :]
+        first = (COLOURS + 12 * view) // 8
+        last = (COLOURS + 12 * view + 11) // 8
+        pieces = list(range(5)) + list(range(first, last + 1))
         found = {piece: jnp.zeros((8, 128), f32) for piece in pieces}
         for owner in range(OWNERS):
             here = block == 4 * owner
@@ -175,21 +244,21 @@
     for group in range(GROUPS):
         view, half = divmod(group, 2)
         for k in range(3):
-            start = SEND * group + 4 * (GEOMETRY + 3 * view + k)
+            start = SEND * group + COLOURS + 4 * (3 * view + k)
             value = jnp.sum(found_ref[pl.ds(start, 4), :], axis=0, keepdims=True)
             colour_ref[pl.ds(8 * view + k, 1), pl.ds(128 * half, 128)] = value
 
-    place = iota((GROUPS, 128), 0)
-    camera = [per_view([camera_ref[view, i] for view in range(VIEWS)]) for i in range(8)]
+    camera = [cast_ref[pl.ds(8 * i, GROUPS), :] for i in range(8)]
     affine = (camera[0:3], camera[3:6])
     centre = [entry_row(i) for i in range(3)]
     scale = [jnp.exp(entry_row(3 + i)) for i in range(3)]
-    raw = [entry_row(6 + i) for i in range(4)]
-    logit = entry_row(10)
+    ratio = [entry_row(6 + i) for i in range(3)]
+    logit = entry_row(9)
     inverse_norm = 1.0 / jnp.sqrt(
-        raw[0] * raw[0] + raw[1] * raw[1] + raw[2] * raw[2] + raw[3] * raw[3]
+        1.0 + ratio[0] * ratio[0] + ratio[1] * ratio[1] + ratio[2] * ratio[2]
     )
-    qw, qx, qy, qz = [component * inverse_norm for component in raw]
+    qw = inverse_norm
+    qx, qy, qz = [component * inverse_norm for component in ratio]
     rotation = [
         [1.0 - 2.0 * (qy * qy + qz * qz), 2.0 * (qx * qy - qw * qz), 2.0 * (qx * qz + qw * qy)],
         [2.0 * (qx * qy + qw * qz), 1.0 - 2.0 * (qx * qx + qz * qz), 2.0 * (qy * qz - qw * qx)],
@@ -203,23 +272,19 @@
     cov_b = sum(screen[0][j] * screen[1][j] for j in range(3))
     cov_c = sum(screen[1][j] * screen[1][j] for j in range(3)) + 0.3
     inverse_det = 1.0 / (cov_a * cov_c - cov_b * cov_b)
-    position = (place & 1) * 128 + iota((GROUPS, 128), 1)
-    live = position < per_view([counts_ref[view, 0] for view in range(VIEWS)])
+    live = cast_ref[pl.ds(64, GROUPS), :] > 0.5
     conic = [
         jnp.where(live, value * inverse_det, 0.0) for value in (cov_c, -cov_b, cov_a)
     ]
     mean = [sum(affine[k][i] * centre[i] for i in range(3)) + camera[6 + k] for k in range(2)]
     opacity = 1.0 / (1.0 + jnp.exp(-logit))
     shown = jnp.where(live, opacity, 0.0)
-    tile = per_view([tiles_ref[view, 0] for view in range(VIEWS)])
-    middle_x = (tile % TILES_WIDE * 16 + 8).astype(f32)
-    middle_y = (tile // TILES_WIDE * 16 + 8).astype(f32)
-    shift_x = mean[0] - middle_x
-    shift_y = mean[1] - middle_y
+    shift_x = mean[0] - cast_ref[pl.ds(72, GROUPS), :]
+    shift_y = mean[1] - cast_ref[pl.ds(80, GROUPS), :]
     kept = (
         [shift_x, shift_y]
         + [(-0.5 * LOG2E) * conic[0], (-LOG2E) * conic[1], (-0.5 * LOG2E) * conic[2]]
-        + [shown, opacity, inverse_norm, qw, qx, qy, qz]
+        + [shown, opacity, qw, qx, qy, qz]
         + conic
         + scale
         + screen[0]
@@ -236,16 +301,12 @@
                 pl.ds(8 * n + half, VIEWS, stride=2), :
             ]
 
-    before = iota((256, 256), 0)
-    after = iota((256, 256), 1)
-    strictly = jnp.where(before < after, 1.0, 0.0).astype(bf16)
-    tri_ref[0:256, :] = strictly
-    tri_ref[256:512, :] = strictly
     offset = iota((16, 256), 0).astype(f32) - 7.5
-    loss_ref[...] = jnp.zeros_like(loss_ref)
-
-    def one_view(view, carry):
-        def row(n):
+    losses = jnp.zeros((8, 128), f32)
+
+    for view in range(VIEWS):
+
+        def row(n, view=view):
             return rows_ref[pl.ds(8 * n + view, 1), :]
 
         mean_u, mean_v = row(0), row(1)
@@ -254,7 +315,7 @@
         along = row(2) * dx * dx
         across = row(3) * dx
         upright = row(4)
-        base = pl.multiple_of(256 * view, 256)
+        base = 256 * view
         for line in range(16):
             dy = (line - 7.5) - mean_v
             exponent = along + (upright * dy * dy + across * dy)
@@ -266,12 +327,12 @@
         for part in range(4):
             rows = pl.ds(64 * part, 64)
             there = pl.ds(base + 64 * part, 64)
-            keep = jnp.exp(nn(logs_ref[rows, :], tri_ref[...]))
+            keep = jnp.exp(nn(logs_ref[rows, :], before_ref[...]))
             keep_ref[there, :] = keep
             high, low = split(jnp.minimum(shade_ref[there, :], 0.99) * keep)
             high_ref[rows, :] = high
             low_ref[rows, :] = low
-        colour = colour_ref[pl.ds(pl.multiple_of(8 * view, 8), 8), :]
+        colour = colour_ref[pl.ds(8 * view, 8), :]
         colour_high, colour_low = [part.astype(f32) for part in split(colour)]
         stacked = jnp.concatenate(
             [
@@ -288,13 +349,11 @@
         residuals = []
         total = jnp.zeros((1, 256), f32)
         for k in range(3):
-            rendered_ref[view, k, :, :] = image[k : k + 1]
+            image_ref[pl.ds(3 * view + k, 1), :] = image[k : k + 1]
             residual = image[k : k + 1] - target_ref[view, k, :, :]
             total = total + residual * residual
             residuals.append(residual * (1.0 / (VIEWS * 256)))
-        loss_ref[...] += jnp.where(
-            iota((8, 128), 1) == view, jnp.sum(total, axis=1, keepdims=True), 0.0
-        )
+        losses = jnp.where(iota((8, 128), 1) == view, jnp.sum(total, axis=1, keepdims=True), losses)
         error = jnp.concatenate(residuals, axis=0)
         error_high, error_low = [part.astype(f32) for part in split(error)]
         pulled = jnp.concatenate(
@@ -302,14 +361,12 @@
         ).astype(bf16)
         tint = nn(pulled, high_ref[...])
         tint_low = nn(pulled, low_ref[...])
-        tint_ref[pl.ds(pl.multiple_of(8 * view, 8), 3), :] = (
+        tint_ref[pl.ds(8 * view, 3), :] = (
             tint[0:3] + tint[3:6] + tint_low[0:3]
         )
-        pulled_ref[pl.ds(pl.multiple_of(16 * view, 16), 16), :] = pulled
-        stacked_ref[pl.ds(pl.multiple_of(16 * view, 16), 16), :] = stacked
-        return carry
-
-    lax.fori_loop(0, VIEWS, one_view, 0)
+        pulled_ref[pl.ds(16 * view, 16), :] = pulled
+        stacked_ref[pl.ds(16 * view, 16), :] = stacked
+    loss_ref[...] = losses
 
 
 def back_kernel(
@@ -318,32 +375,20 @@
     pulled_ref,
     stacked_ref,
     entry_ref,
-    camera_ref,
+    cast_ref,
+    behind_ref,
+    basis_ref,
     grads_ref,
     logs_ref,
     high_ref,
     low_ref,
     moment_ref,
-    tri_ref,
 ):
-    before = iota((256, 256), 0)
-    after = iota((256, 256), 1)
-    strictly = jnp.where(before > after, 1.0, 0.0).astype(bf16)
-    tri_ref[0:256, :] = strictly
-    tri_ref[256:512, :] = strictly
-    pixel = iota((16, 256), 1)
-    power = iota((16, 256), 0)
-    pixel_u = (pixel % 16).astype(f32) - 7.5
-    pixel_v = (pixel // 16).astype(f32) - 7.5
-    basis = jnp.where(power == 0, 1.0, jnp.where(power == 1, pixel_u, pixel_v))
-    basis = jnp.where(power == 3, pixel_u * pixel_u, basis)
-    basis = jnp.where(power == 4, pixel_u * pixel_v, basis)
-    basis = jnp.where(power == 5, pixel_v * pixel_v, basis)
-    basis = jnp.where(power > 5, 0.0, basis).astype(bf16)
-
-    def one_view(view, carry):
-        base = pl.multiple_of(256 * view, 256)
-        small = pl.ds(pl.multiple_of(16 * view, 16), 16)
+    basis = basis_ref[...]
+
+    for view in range(VIEWS):
+        base = 256 * view
+        small = pl.ds(16 * view, 16)
         pull = tn(pulled_ref[small, :], stacked_ref[small, :])
         for part in range(4):
             rows = pl.ds(64 * part, 64)
@@ -355,7 +400,7 @@
         for part in range(4):
             rows = pl.ds(64 * part, 64)
             there = pl.ds(base + 64 * part, 64)
-            behind = nn(logs_ref[rows, :], tri_ref[...])
+            behind = nn(logs_ref[rows, :], behind_ref[...])
             shade = shade_ref[there, :]
             alpha = jnp.minimum(shade, 0.99)
             slope = pull[64 * part : 64 * part + 64] * keep_ref[there, :] - behind / (1.0 - alpha)
@@ -368,18 +413,15 @@
             moment_ref[pl.ds(2 * view + half, 8, stride=8), :] = moments[
                 0:8, 128 * half : 128 * half + 128
             ]
-        return carry
-
-    lax.fori_loop(0, VIEWS, one_view, 0)
 
     kept = [entry_ref[pl.ds(8 * n, GROUPS), :] for n in range(KEPT)]
     shift_x, shift_y = kept[0:2]
-    opacity, inverse_norm, qw, qx, qy, qz = kept[6:12]
-    conic = kept[12:15]
-    scale = kept[15:18]
-    screen = (kept[18:21], kept[21:24])
-    stretched = (kept[24:27], kept[27:30], kept[30:33])
-    camera = [per_view([camera_ref[view, i] for view in range(VIEWS)]) for i in range(6)]
+    opacity, qw, qx, qy, qz = kept[6:11]
+    conic = kept[11:14]
+    scale = kept[14:17]
+    screen = (kept[17:20], kept[20:23])
+    stretched = (kept[23:26], kept[26:29], kept[29:32])
+    camera = [cast_ref[pl.ds(8 * i, GROUPS), :] for i in range(6)]
     affine = (camera[0:3], camera[3:6])
     m_0, m_u, m_v, m_uu, m_uv, m_vv = [
         moment_ref[pl.ds(8 * n, GROUPS), :] for n in range(6)
@@ -436,7 +478,7 @@
     gradients = (
         [affine[0][i] * d_mean[0] + affine[1][i] * d_mean[1] for i in range(3)]
         + d_scale
-        + [(d_unit[i] - unit[i] * radial) * inverse_norm for i in range(4)]
+        + [(d_unit[i] - unit[i] * radial) * qw for i in range(1, 4)]
         + [m_0 * (1.0 - opacity)]
     )
     for n, value in enumerate(gradients):
@@ -446,7 +488,8 @@
 
 
 def scatter_kernel(
-    lists_ref,
+    places_ref,
+    chosen_ref,
     grads_ref,
     tint_ref,
     loss_ref,
@@ -455,18 +498,12 @@
     across_ref,
     back_ref,
     spread_ref,
-    places_ref,
 ):
-    coarse = iota((32, 128), 0)
-    fine = iota((256, 128), 0)
     kinds_of = GEOMETRY * 32
     for group in range(GROUPS):
         view, half = divmod(group, 2)
-        local = lists_ref[view, :, 128 * half : 128 * half + 128] & 8191
         lanes = pl.ds(128 * group, 128)
-        places_ref[:, lanes] = jnp.where((local & 255) == fine, 1.0, 0.0).astype(bf16)
-        owner_part = ((local >> 8) & 1) * 16 + (local >> 9)
-        chosen = jnp.where(owner_part == coarse, 1.0, 0.0).astype(bf16)
+        chosen = chosen_ref[:, lanes]
         for n in range(GEOMETRY):
             for part in range(2):
                 value = grads_ref[pl.ds(16 * n + 8 * part + group, 1), :]
@@ -486,7 +523,7 @@
     def store(row, value):
         for upper in range(2):
             for side in range(2):
-                back_ref[pl.ds(4 * row + 2 * upper + side, 16, stride=BACK), :] = value[
+                back_ref[pl.ds(4 * row + 2 * upper + side, 16, stride=SEND), :] = value[
                     16 * upper : 16 * upper + 16, 128 * side : 128 * side + 128
                 ]
 
@@ -502,30 +539,45 @@
                 dense[32 * k : 32 * k + 32] + dense[96 + 32 * k : 96 + 32 * k + 32],
             )
     for owner in range(OWNERS):
-        back_ref[pl.ds(BACK * owner + SEND, 8), :] = losses
+        back_ref[pl.ds(SEND * owner + ERRORS, 4), :] = losses[0:4]
 
 
 def fold_kernel(back_ref, total_ref, loss_ref):
-    total = back_ref[0:BACK, :]
+    total = back_ref[0:SEND, :]
     for owner in range(1, OWNERS):
-        total = total + back_ref[pl.ds(BACK * owner, BACK), :]
-    total_ref[...] = total[0:SEND]
-    loss_ref[...] = total[SEND:BACK]
+        total = total + back_ref[pl.ds(SEND * owner, SEND), :]
+    total_ref[...] = total
+    loss_ref[...] = total[SEND - 8 : SEND]
 
 
 def adam_kernel(
     total_ref,
     slope_ref,
+    column_ref,
+    image_ref,
     params_ref,
     moment_one_ref,
     moment_two_ref,
-    camera_ref,
+    params_hbm,
+    first_hbm,
+    second_hbm,
+    rendered_hbm,
+    gradient_ref,
     params_out,
     first_out,
     second_out,
-    gradient_ref,
+    rendered_out,
+    sems,
 ):
-    columns = [harmonic_halves(camera_ref, view) for view in range(VIEWS)]
+    for view in range(VIEWS):
+        for k in range(3):
+            rendered_out[view, k, :, :] = image_ref[pl.ds(3 * view + k, 1), :]
+    copies = [pltpu.make_async_copy(rendered_out, rendered_hbm, sems.at[0])]
+    copies[0].start()
+    columns = [
+        [column_ref[pl.ds(16 * view + 8 * half, 8), :] for half in range(2)]
+        for view in range(VIEWS)
+    ]
     row = iota((59, 128), 0)
     rates = jnp.where(row < 14, 0.0025, 0.000125)
     rates = jnp.where(row < 11, 0.05, rates)
@@ -535,13 +587,18 @@
     for quarter in range(4):
         lanes = pl.ds(128 * quarter, 128)
         base = 64 * quarter
-        gradient_ref[pl.ds(base, 8), :] = total_ref[pl.ds(quarter, 8, stride=4), :]
-        gradient_ref[pl.ds(base + 8, 3), :] = total_ref[pl.ds(32 + quarter, 3, stride=4), :]
+        gradient_ref[pl.ds(base, 6), :] = total_ref[pl.ds(quarter, 6, stride=4), :]
+        w = params_ref[6:7, lanes]
+        d_ratio = total_ref[pl.ds(24 + quarter, 3, stride=4), :] / w
+        lean = jnp.sum(d_ratio * params_ref[7:10, lanes], axis=0, keepdims=True)
+        gradient_ref[pl.ds(base + 6, 1), :] = -lean / w
+        gradient_ref[pl.ds(base + 7, 3), :] = d_ratio
+        gradient_ref[pl.ds(base + 10, 1), :] = total_ref[pl.ds(36 + quarter, 1), :]
         for k in range(3):
             tints = []
             for view in range(VIEWS):
-                row = 4 * (3 * view + k) + quarter
-                tint = total_ref[pl.ds(4 * GEOMETRY + row, 1), :] * slope_ref[pl.ds(row, 1), :]
+                place = 4 * (3 * view + k) + quarter
+                tint = total_ref[pl.ds(COLOURS + place, 1), :] * slope_ref[pl.ds(place, 1), :]
                 tints.append(jnp.broadcast_to(tint, (8, 128)))
             for half in range(2):
                 gradient_ref[pl.ds(base + 11 + 24 * half + k, 8, stride=3), :] = sum(
@@ -553,10 +610,20 @@
         first_out[:, lanes] = first
         second_out[:, lanes] = second
         params_out[:, lanes] = params_ref[:, lanes] - rates * first / (jnp.sqrt(second) + 1e-15)
+        pairs = ((params_out, params_hbm), (first_out, first_hbm), (second_out, second_hbm))
+        for n, (source, target) in enumerate(pairs):
+            copy = pltpu.make_async_copy(
+                source.at[:, lanes], target.at[:, lanes], sems.at[1 + 3 * quarter + n]
+            )
+            copy.start()
+            copies.append(copy)
+    for copy in copies:
+        copy.wait()
 
 
 VM = pl.BlockSpec(memory_space=pltpu.VMEM)
 SM = pl.BlockSpec(memory_space=pltpu.SMEM)
+HB = pl.BlockSpec(memory_space=pltpu.HBM)
 
 
 def shape(*dims):
@@ -565,6 +632,10 @@
 
 def swapped(value, partner):
     return lax.ppermute(value, GAUSS, [(i, partner(i)) for i in range(8)])
+
+
+def in_hbm(array):
+    return pltpu.with_memory_space_constraint(array, pltpu.HBM)
 
 
 def limit(mib):
@@ -575,19 +646,47 @@
     sent, slope = pl.pallas_call(
         pack_kernel,
         out_shape=(shape(OWNERS * SEND, 128), shape(36, 128)),
-        in_specs=[VM, SM],
+        in_specs=[HB, HB],
         out_specs=(VM, VM),
-        scratch_shapes=[pltpu.VMEM((SEND, 128), f32), pltpu.VMEM((256, 128), f32)],
+        scratch_shapes=[
+            pltpu.VMEM((59, 512), f32),
+            pltpu.VMEM((SEND, 128), f32),
+            pltpu.VMEM((256, 128), f32),
+            pltpu.SMEM((3, 11), f32),
+            pltpu.SemaphoreType.DMA((2,)),
+        ],
+        compiler_params=limit(4),
         name="pack",
-    )(params, camera)
+    )(in_hbm(params), in_hbm(camera))
     table = lax.all_to_all(
         sent.reshape(OWNERS, SEND, 128), TILE, split_axis=0, concat_axis=0, tiled=True
     ).reshape(OWNERS * SEND, 128)
+    late = lax.optimization_barrier((slope, splat_lists, counts, tile_ids, camera))
+    slope = late[0]
+    lane, block, cast, column, places, chosen, before, behind, basis = pl.pallas_call(
+        prepare_kernel,
+        out_shape=(
+            jax.ShapeDtypeStruct((48, 128), jnp.int32),
+            jax.ShapeDtypeStruct((48, 128), jnp.int32),
+            shape(88, 128),
+            shape(48, 128),
+            jax.ShapeDtypeStruct((256, 768), bf16),
+            jax.ShapeDtypeStruct((32, 768), bf16),
+            jax.ShapeDtypeStruct((512, 256), bf16),
+            jax.ShapeDtypeStruct((512, 256), bf16),
+            jax.ShapeDtypeStruct((16, 256), bf16),
+        ),
+        in_specs=[VM, SM, SM, SM],
+        out_specs=(VM,) * 9,
+        compiler_params=limit(4),
+        cost_estimate=pl.CostEstimate(flops=1 << 28, bytes_accessed=1 << 20, transcendentals=0),
+        name="prepare",
+    )(*late[1:])
     half = jax.ShapeDtypeStruct((48, 256), bf16)
-    rendered, loss, shade, keep, pulled, stacked, tint, entries = pl.pallas_call(
+    image, loss, shade, keep, pulled, stacked, tint, entries = pl.pallas_call(
         front_kernel,
         out_shape=(
-            shape(VIEWS, 3, 1, 256),
+            shape(16, 256),
             shape(8, 128),
             shape(VIEWS * 256, 256),
             shape(VIEWS * 256, 256),
@@ -596,7 +695,7 @@
             shape(24, 256),
             shape(8 * KEPT, 128),
         ),
-        in_specs=[VM, VM, SM, SM, SM, VM],
+        in_specs=[VM] * 6,
         out_specs=(VM,) * 8,
         scratch_shapes=[
             pltpu.VMEM((GROUPS * SEND, 128), f32),
@@ -605,47 +704,42 @@
             pltpu.VMEM((256, 512), bf16),
             pltpu.VMEM((256, 256), bf16),
             pltpu.VMEM((256, 256), bf16),
-            pltpu.VMEM((512, 256), bf16),
         ],
         compiler_params=limit(16),
         name="front",
-    )(table, splat_lists, counts, tile_ids, camera, target)
+    )(table, lane, block, cast, before, target)
     core = swapped(loss, lambda i: i ^ 1)
     side = swapped(loss, lambda i: i ^ 2)
     across = swapped(loss, lambda i: i ^ 3)
     grads = pl.pallas_call(
         back_kernel,
         out_shape=shape(16 * GEOMETRY, 128),
-        in_specs=[VM, VM, VM, VM, VM, SM],
+        in_specs=[VM] * 8,
         out_specs=VM,
         scratch_shapes=[
             pltpu.VMEM((256, 512), bf16),
             pltpu.VMEM((256, 256), bf16),
             pltpu.VMEM((256, 256), bf16),
             pltpu.VMEM((64, 128), f32),
-            pltpu.VMEM((512, 256), bf16),
         ],
         compiler_params=limit(12),
         cost_estimate=pl.CostEstimate(
             flops=1 << 31, bytes_accessed=1 << 23, transcendentals=1 << 20
         ),
         name="back",
-    )(shade, keep, pulled, stacked, entries, camera)
+    )(shade, keep, pulled, stacked, entries, cast, behind, basis)
     back = pl.pallas_call(
         scatter_kernel,
-        out_shape=shape(OWNERS * BACK, 128),
-        in_specs=[VM] * 7,
+        out_shape=shape(OWNERS * SEND, 128),
+        in_specs=[VM] * 8,
         out_specs=VM,
-        scratch_shapes=[
-            pltpu.VMEM((2 * 32 * GEOMETRY + 192, 768), bf16),
-            pltpu.VMEM((256, 768), bf16),
-        ],
+        scratch_shapes=[pltpu.VMEM((2 * 32 * GEOMETRY + 192, 768), bf16)],
         compiler_params=limit(12),
         name="scatter",
-    )(splat_lists, grads, tint, loss, core, side, across)
+    )(places, chosen, grads, tint, loss, core, side, across)
     arrived = lax.all_to_all(
-        back.reshape(OWNERS, BACK, 128), TILE, split_axis=0, concat_axis=0, tiled=True
-    ).reshape(OWNERS * BACK, 128)
+        back.reshape(OWNERS, SEND, 128), TILE, split_axis=0, concat_axis=0, tiled=True
+    ).reshape(OWNERS * SEND, 128)
     total, loss = pl.pallas_call(
         fold_kernel,
         out_shape=(shape(SEND, 128), shape(8, 128)),
@@ -655,19 +749,27 @@
         name="fold",
     )(arrived)
     other = swapped(loss, lambda i: 6 - (i & 6) + (i & 1))
-    updated, first, second = pl.pallas_call(
+    wide = shape(59, 512)
+    updated, first, second, rendered = pl.pallas_call(
         adam_kernel,
-        out_shape=(shape(59, 512), shape(59, 512), shape(59, 512)),
-        in_specs=[VM, VM, VM, VM, VM, SM],
-        out_specs=(VM, VM, VM),
-        scratch_shapes=[pltpu.VMEM((256, 128), f32)],
+        out_shape=(wide, wide, wide, shape(VIEWS, 3, 1, 256)),
+        in_specs=[VM] * 7,
+        out_specs=(HB,) * 4,
+        scratch_shapes=[
+            pltpu.VMEM((256, 128), f32),
+            pltpu.VMEM((59, 512), f32),
+            pltpu.VMEM((59, 512), f32),
+            pltpu.VMEM((59, 512), f32),
+            pltpu.VMEM((VIEWS, 3, 1, 256), f32),
+            pltpu.SemaphoreType.DMA((13,)),
+        ],
         compiler_params=limit(4),
         cost_estimate=pl.CostEstimate(
             flops=1 << 30, bytes_accessed=1 << 22, transcendentals=1 << 16
         ),
         name="adam",
-    )(total, slope, params, moment_one, moment_two, camera)
-    losses = (loss + other)[0, :VIEWS] * (0.5 / (3 * 256 * 128))
+    )(total, slope, column, image, params, moment_one, moment_two)
+    losses = (loss + other)[4, :VIEWS] * (0.5 / (3 * 256 * 128))
     return (updated, first, second, rendered, losses)
 
 

time: 55.2 us -> 53.2 us (0.964)
  Pallas kernels: 10.2 us -> 8.5 us
  starting transfers between devices: 12.9 us -> 12 us
    ppermute x4, waiting for transfers between devices: 0.61 us -> 2.31 us  [swapped(): return lax.ppermute(value, GAUSS, [(i, partner(i)) for i in range(8)])]
    all_to_all x1, waiting for transfers between devices: 12.7 us -> 11.4 us  [shards(): lax.all_to_all(sent.reshape(OWNERS, SEND, 128), TILE, split_axis=0, conca...]
    pallas_call x1, Pallas kernels: 2.42 us -> 1.36 us  [shards(): pl.pallas_call(back_kernel, out_shape=shape(16 * GEOMETRY, 128), in_specs...]
    ppermute x4, starting transfers between devices: 4.73 us -> 3.96 us  [swapped(): return lax.ppermute(value, GAUSS, [(i, partner(i)) for i in range(8)])]
    pallas_call x3 -> x4, Pallas kernels: 5.85 us -> 5.23 us  [the longest x1 2.86 us: shards(): pl.pallas_call(front_kernel, out_shape=(shape(16, 256), shape(8, 128), sh...]
  transfers between devices with their start and end apart: 5 -> 5, of which waited for: 2 -> 3; matrix products, arithmetic and copies ran while one was open for 0% -> 0% of each run, Pallas kernels for 7% -> 6%
where the time goes in v2:
time: 53.2 us; the launch traced here: 52.9 us
  blocking collectives  16.7 us (31%)
  waiting for transfers between devices  13.7 us (26%)
  starting transfers between devices  12 us (23%)
  Pallas kernels  8.5 us (16%)
  between operations  0.74 us (1%)
  local copies, waits for them, and re-layouts  0.71 us (1%)
    all_to_all x1, blocking collectives, shards(): lax.all_to_all(back.reshape(OWNERS, SEND, 128), TILE, split_axis=0, conca...  16.7 us
    all_to_all x1, waiting for transfers between devices, shards(): lax.all_to_all(sent.reshape(OWNERS, SEND, 128), TILE, split_axis=0, conca...  11.4 us
    all_to_all x1, starting transfers between devices, shards(): lax.all_to_all(sent.reshape(OWNERS, SEND, 128), TILE, split_axis=0, conca...  8 us
    ppermute x4, starting transfers between devices, swapped(): return lax.ppermute(value, GAUSS, [(i, partner(i)) for i in range(8)])  3.96 us
    pallas_call x1, Pallas kernels, shards(): pl.pallas_call(front_kernel, out_shape=(shape(16, 256), shape(8, 128), sh...  2.86 us
    ppermute x4, waiting for transfers between devices, swapped(): return lax.ppermute(value, GAUSS, [(i, partner(i)) for i in range(8)])  2.31 us
    pallas_call x1, Pallas kernels, shards(): pl.pallas_call(pack_kernel, out_shape=(shape(OWNERS * SEND, 128), shape(3...  1.88 us
    pallas_call x1, Pallas kernels, shards(): pl.pallas_call(back_kernel, out_shape=shape(16 * GEOMETRY, 128), in_specs...  1.36 us
  transfers between devices with their start and end apart: 5, of which 3 were waited for; matrix products, arithmetic and copies ran while one was open for 0% of the time, Pallas kernels for 6%

profile of v2, /device:TPU:0, one launch (start us, length us, event | category | flops | bytes accessed | tf_op | source)
XLA Modules:
  0.0 52.9 jit_solution(6269615661632844522)
XLA Ops:
  0.6 1.9 %pack.1 = (f32[1280,128]{1,0:T(8,128)}, f32[36,128]{1,0:T(8,128)S(1)}) custom-call(f32[59,512]{1,0:T(8,128)} %params_ref.1, f32[3,11]{1,0:T(4,128)} %camera_ref), custom_call_target="tpu_custom_call" | custom-call | tf_op jit(solution)/shard_map/pack/pallas_call | solution.py:646
  2.5 0.0 copy-start.6
  2.5 0.0 copy-start.7
  2.5 8.0 %all-to-all-start = ((f32[16,80,128]{2,1,0:T(8,128)}), f32[16,80,128]{2,1,0:T(8,128)S(1)}, u32[]{:S(2)}, u32[]{:S(2)}) async-start(f32[16,80,128]{2,1,0:T(8,128)} %bitcast), calls=%async_computation | async-start | bytes 1310720 | tf_op jit(solution)/shard_map/all_to_all | solution.py:661
  10.5 0.0 copy-start.5
  10.6 0.0 copy-start.2
  10.6 0.1 copy.13.counts_ref
  10.7 0.1 copy.14.tiles_ref
  10.8 0.5 copy-done.5
  11.2 0.0 copy-done.2
  11.3 0.8 %prepare.1 = (s32[48,128]{1,0:T(8,128)S(1)}, s32[48,128]{1,0:T(8,128)S(1)}, f32[88,128]{1,0:T(8,128)S(1)}, f32[48,128]{1,0:T(8,128)S(1)}, bf16[256,768]{1,0:T(8,...) custom-call(s32[3,1,256]{2,1,0:T(1,128)S(1)} %copy-done.5, ...), custom_call_target="tpu_custom_call" | custom-call | flops 268435456 | bytes 1048576 | tf_op jit(solution)/shard_map/prepare/pallas_call | solution.py:666
  12.1 0.0 copy-start.1
  12.1 11.4 %all-to-all-done = f32[16,80,128]{2,1,0:T(8,128)S(1)} async-done(((f32[16,80,128]{2,1,0:T(8,128)}), f32[16,80,128]{2,1,0:T(8,128)S(1)}, u32[]{:S(2)}, u32[]{:S(2)}) %all-to-all-start) | async-done | bytes 655392 | tf_op jit(solution)/shard_map/all_to_all | solution.py:661
  23.5 2.9 %front.1 = (f32[16,256]{1,0:T(8,128)S(1)}, f32[8,128]{1,0:T(8,128)S(1)}, f32[768,256]{1,0:T(8,128)S(1)}, f32[768,256]{1,0:T(8,128)S(1)}, bf16[48,256]{1,0:T(8,12...) custom-call(f32[1280,128]{1,0:T(8,128)S(1)} %bitcast.6, ...), custom_call_target="tpu_custom_call" | custom-call | tf_op jit(solution)/shard_map/front/pallas_call | solution.py:686
  26.4 1.6 %collective-permute-start.1 = (f32[8,128]{1,0:T(8,128)S(1)}, f32[8,128]{1,0:T(8,128)S(1)}, u32[]{:S(2)}, u32[]{:S(2)}) collective-permute-start(f32[8,128]{1,0:T(8,128)S(1)} %get-tuple-element.55.loss_ref), channel_id=1, source_target_pairs={{0,32},{16,48},{32,0},{48,16},{64,96},{80,112},{96,64},{112,80},{1... | collective-permute-start | bytes 12296 | tf_op jit(solution)/shard_map/ppermute | solution.py:634
  28.0 0.2 collective-permute-start
  28.2 1.4 %back.1.grads_ref = f32[160,128]{1,0:T(8,128)S(1)} custom-call(f32[768,256]{1,0:T(8,128)S(1)} %get-tuple-element.47.shade_ref, f32[768,256]{1,0:T(8,128)S(1)} %get-tuple-element.48.keep_ref, bf16[48,256]{1,0:T(8,128)(2,1)S(1)} %get-tuple-element.49.pulled_ref, bf16[48,256]{1,0:T(8,128)(2,1)S(1)} %get-tuple-element.50.stacked_ref, ...), custom_call_target="tpu_custom_call" | custom-call | flops 2147483648 | bytes 8388608 | tf_op jit(solution)/shard_map/back/pallas_call | solution.py:714
  29.6 0.4 collective-permute-done.1.side_ref
  30.0 0.7 %scatter.1 = f32[1280,128]{1,0:T(8,128)S(1)} custom-call(bf16[256,768]{1,0:T(8,128)(2,1)S(1)} %get-tuple-element.40.places_ref, bf16[32,768]{1,0:T(8,128)(2,1)S(1)} %get-tuple-element.41.chosen_ref, f32[160,128]{1,0:T(8,128)S(1)} %back.1.grads_ref, f32[24,256]{1,0:T(8,128)S(1)} %get-tuple-element.54.tint_ref, f32[8,128]{1,0:T(8,128)S(1)} %get-tuple-element.55.loss_ref, ...), custom_call_target="tpu_custom_call" | custom-call | tf_op jit(solution)/shard_map/scatter/pallas_call | solution.py:731
  30.7 16.7 %all_to_all.10 = f32[16,80,128]{2,1,0:T(8,128)S(1)} all-to-all(f32[16,80,128]{2,1,0:T(8,128)S(1)} %bitcast.7), channel_id=1, replica_groups=mesh['gauss_0'=4,'gauss_1'=2,'tile_0'=4,'tile_1'=4] {'tile_0','tile_1'}, dimensions={0} | all-to-all | bytes 1310720 | tf_op jit(solution)/shard_map/all_to_all | solution.py:740
  47.5 2.1 %collective-permute-start.3 = (f32[8,128]{1,0:T(8,128)S(1)}, f32[8,128]{1,0:T(8,128)S(1)}, u32[]{:S(2)}, u32[]{:S(2)}) collective-permute-start(f32[8,128]{1,0:T(8,128)S(1)} %get-tuple-element.64), channel_id=1, source_target_pairs={{0,96},{16,112},{32,64},{48,80},{64,32},{80,48},{96,0},{112,16},{1... | collective-permute-start | bytes 12296 | tf_op jit(solution)/shard_map/ppermute | solution.py:634
  49.6 0.9 %adam.1 = (f32[59,512]{1,0:T(8,128)}, f32[59,512]{1,0:T(8,128)}, f32[59,512]{1,0:T(8,128)}, f32[3,3,1,256]{3,2,1,0:T(1,128)}) custom-call(f32[80,128]{1,0:T(8,128)S(1)} %get-tuple-element.56.total_ref, f32[36,128]{1,0:T(8,128)S(1)} %get-tuple-element.57.slope_ref, f32[48,128]{1,0:T(8,128)S(1)} %get-tuple-element.58.column_ref, ...), custom_call_target="tpu_custom_call" | custom-call | flops 1073741824 | bytes 4194304 | tf_op jit(solution)/shard_map/adam/pallas_call | solution.py:753
  50.5 1.9 %collective-permute-done.3 = f32[8,128]{1,0:T(8,128)S(1)} collective-permute-done((f32[8,128]{1,0:T(8,128)S(1)}, f32[8,128]{1,0:T(8,128)S(1)}, u32[]{:S(2)}, u32[]{:S(2)}) %collective-permute-start.3) | collective-permute-done | bytes 4128 | tf_op jit(solution)/shard_map/ppermute | solution.py:634
  52.4 0.5 multiply_bitcast_fusion
  (14 shorter events, 0.1 us)
Async XLA Ops:
  2.5 8.0 %copy-start.6 = (s32[3,1]{0,1:T(1,128)S(1)}, s32[3,1]{0,1:T(1,128)}, u32[]{:S(2)}) copy-start(s32[3,1]{0,1:T(1,128)} %param.15) | copy-start | bytes 40
  2.5 8.2 %copy-start.7 = (s32[3,1]{0,1:T(1,128)S(1)}, s32[3,1]{0,1:T(1,128)}, u32[]{:S(2)}) copy-start(s32[3,1]{0,1:T(1,128)} %param.13) | copy-start | bytes 40
  2.5 20.9 %all-to-all-start = ((f32[16,80,128]{2,1,0:T(8,128)}), f32[16,80,128]{2,1,0:T(8,128)S(1)}, u32[]{:S(2)}, u32[]{:S(2)}) async-start(f32[16,80,128]{2,1,0:T(8,128)} %bitcast), calls=%async_computation | async-start | bytes 1310720 | tf_op jit(solution)/shard_map/all_to_all | solution.py:661
  10.5 0.7 %copy-start.5 = (s32[3,1,256]{2,1,0:T(1,128)S(1)}, s32[3,1,256]{2,1,0:T(1,128)}, u32[]{:S(2)}) copy-start(s32[3,1,256]{2,1,0:T(1,128)} %lists_ref) | copy-start | bytes 9220
  10.6 0.7 %copy-start.2 = (f32[3,11]{1,0:T(4,128)S(1)}, f32[3,11]{1,0:T(4,128)}, u32[]{:S(2)}) copy-start(f32[3,11]{1,0:T(4,128)} %camera_ref) | copy-start | bytes 400
  12.1 11.4 %copy-start.1 = (f32[3,3,1,256]{3,2,1,0:T(1,128)S(1)}, f32[3,3,1,256]{3,2,1,0:T(1,128)}, u32[]{:S(2)}) copy-start(f32[3,3,1,256]{3,2,1,0:T(1,128)} %target_ref.1) | copy-start | bytes 27652
  26.3 3.2 %collective-permute-start.2 = (f32[8,128]{1,0:T(8,128)S(1)}, f32[8,128]{1,0:T(8,128)S(1)}, u32[]{:S(2)}, u32[]{:S(2)}) collective-permute-start(f32[8,128]{1,0:T(8,128)S(1)} %get-tuple-element.55.loss_ref), channel_id=1, source_target_pairs={{0,48},{16,32},{32,16},{48,0},{64,112},{80,96},{96,80},{112,64},{1... | collective-permute-start | bytes 12296 | tf_op jit(solution)/shard_map/ppermute | solution.py:634
  26.4 3.7 %collective-permute-start.1 = (f32[8,128]{1,0:T(8,128)S(1)}, f32[8,128]{1,0:T(8,128)S(1)}, u32[]{:S(2)}, u32[]{:S(2)}) collective-permute-start(f32[8,128]{1,0:T(8,128)S(1)} %get-tuple-element.55.loss_ref), channel_id=1, source_target_pairs={{0,32},{16,48},{32,0},{48,16},{64,96},{80,112},{96,64},{112,80},{1... | collective-permute-start | bytes 12296 | tf_op jit(solution)/shard_map/ppermute | solution.py:634
  28.0 2.0 %collective-permute-start = (f32[8,128]{1,0:T(8,128)S(1)}, f32[8,128]{1,0:T(8,128)S(1)}, u32[]{:S(2)}, u32[]{:S(2)}) collective-permute-start(f32[8,128]{1,0:T(8,128)S(1)} %get-tuple-element.55.loss_ref), channel_id=1, source_target_pairs={{0,16},{16,0},{32,48},{48,32},{64,80},{80,64},{96,112},{112,96},{1... | collective-permute-start | bytes 12296 | tf_op jit(solution)/shard_map/ppermute | solution.py:634
  47.4 2.1 %copy-start = (f32[59,512]{1,0:T(8,128)S(1)}, f32[59,512]{1,0:T(8,128)}, u32[]{:S(2)}) copy-start(f32[59,512]{1,0:T(8,128)} %params_ref.1) | copy-start | bytes 362500
  47.4 2.1 %copy-start.3 = (f32[59,512]{1,0:T(8,128)S(1)}, f32[59,512]{1,0:T(8,128)}, u32[]{:S(2)}) copy-start(f32[59,512]{1,0:T(8,128)} %moment_one_ref.1) | copy-start | bytes 362500
  47.4 2.1 %copy-start.4 = (f32[59,512]{1,0:T(8,128)S(1)}, f32[59,512]{1,0:T(8,128)}, u32[]{:S(2)}) copy-start(f32[59,512]{1,0:T(8,128)} %moment_two_ref.1) | copy-start | bytes 362500
  47.5 4.9 %collective-permute-start.3 = (f32[8,128]{1,0:T(8,128)S(1)}, f32[8,128]{1,0:T(8,128)S(1)}, u32[]{:S(2)}, u32[]{:S(2)}) collective-permute-start(f32[8,128]{1,0:T(8,128)S(1)} %get-tuple-element.64), channel_id=1, source_target_pairs={{0,96},{16,112},{32,64},{48,80},{64,32},{80,48},{96,0},{112,16},{1... | collective-permute-start | bytes 12296 | tf_op jit(solution)/shard_map/ppermute | solution.py:634

commit v3 on v2

--- a/solution.py
+++ b/solution.py
@@ -85,18 +85,91 @@
 
 
 def pack_kernel(
-    params_hbm, camera_hbm, send_ref, slope_ref, params_ref, pack_ref, tall_ref, camera_ref, sems
+    params_hbm,
+    camera_hbm,
+    lists_hbm,
+    counts_hbm,
+    tiles_hbm,
+    send_ref,
+    slope_ref,
+    lane_ref,
+    block_ref,
+    cast_ref,
+    column_ref,
+    places_ref,
+    chosen_ref,
+    before_ref,
+    behind_ref,
+    basis_ref,
+    params_ref,
+    pack_ref,
+    tall_ref,
+    camera_ref,
+    lists_ref,
+    counts_ref,
+    tiles_ref,
+    sems,
 ):
+    sources = [camera_hbm, counts_hbm, tiles_hbm, lists_hbm]
+    targets = [camera_ref, counts_ref, tiles_ref, lists_ref]
+    for quarter in range(4):
+        lanes = pl.ds(128 * quarter, 128)
+        sources.append(params_hbm.at[:, lanes])
+        targets.append(params_ref.at[:, lanes])
     copies = [
-        pltpu.make_async_copy(camera_hbm, camera_ref, sems.at[0]),
-        pltpu.make_async_copy(params_hbm, params_ref, sems.at[1]),
+        pltpu.make_async_copy(source, target, sems.at[n])
+        for n, (source, target) in enumerate(zip(sources, targets))
     ]
     for copy in copies:
         copy.start()
-    copies[0].wait()
+
+    first = iota((256, 256), 0)
+    second = iota((256, 256), 1)
+    for ref, strictly in ((before_ref, first < second), (behind_ref, first > second)):
+        ones = jnp.where(strictly, 1.0, 0.0).astype(bf16)
+        ref[0:256, :] = ones
+        ref[256:512, :] = ones
+    pixel = iota((16, 256), 1)
+    power = iota((16, 256), 0)
+    pixel_u = (pixel % 16).astype(f32) - 7.5
+    pixel_v = (pixel // 16).astype(f32) - 7.5
+    basis = jnp.where(power == 0, 1.0, jnp.where(power == 1, pixel_u, pixel_v))
+    basis = jnp.where(power == 3, pixel_u * pixel_u, basis)
+    basis = jnp.where(power == 4, pixel_u * pixel_v, basis)
+    basis = jnp.where(power == 5, pixel_v * pixel_v, basis)
+    basis_ref[...] = jnp.where(power > 5, 0.0, basis).astype(bf16)
+    for copy in copies[0:4]:
+        copy.wait()
     columns = [harmonic_halves(camera_ref, view) for view in range(VIEWS)]
-    copies[1].wait()
+    quarter = iota((8, 128), 0) & 3
+    fine = iota((256, 128), 0)
+    coarse = iota((32, 128), 0)
+    for group in range(GROUPS):
+        view, half = divmod(group, 2)
+        local = lists_ref[view, :, 128 * half : 128 * half + 128] & 8191
+        spread = jnp.broadcast_to(local, (8, 128))
+        lane_ref[pl.ds(8 * group, 8), :] = spread & 127
+        block_ref[pl.ds(8 * group, 8), :] = (spread >> 7) - quarter
+        lanes = pl.ds(128 * group, 128)
+        places_ref[:, lanes] = jnp.where((local & 255) == fine, 1.0, 0.0).astype(bf16)
+        owner_part = ((local >> 8) & 1) * 16 + (local >> 9)
+        chosen_ref[:, lanes] = jnp.where(owner_part == coarse, 1.0, 0.0).astype(bf16)
+    for i in range(8):
+        cast_ref[pl.ds(8 * i, GROUPS), :] = per_view(
+            [camera_ref[view, i] for view in range(VIEWS)]
+        )
+    place = iota((GROUPS, 128), 0)
+    position = (place & 1) * 128 + iota((GROUPS, 128), 1)
+    live = position < per_view([counts_ref[0, view] for view in range(VIEWS)])
+    cast_ref[pl.ds(64, GROUPS), :] = jnp.where(live, 1.0, 0.0)
+    tile = per_view([tiles_ref[0, view] for view in range(VIEWS)])
+    cast_ref[pl.ds(72, GROUPS), :] = (tile % TILES_WIDE * 16 + 8).astype(f32)
+    cast_ref[pl.ds(80, GROUPS), :] = (tile // TILES_WIDE * 16 + 8).astype(f32)
+    for view in range(VIEWS):
+        for half in range(2):
+            column_ref[pl.ds(16 * view + 8 * half, 8), :] = columns[view][half]
     for quarter in range(4):
+        copies[4 + quarter].wait()
         lanes = pl.ds(128 * quarter, 128)
         pack_ref[pl.ds(quarter, 6, stride=4), :] = params_ref[0:6, lanes]
         pack_ref[pl.ds(24 + quarter, 3, stride=4), :] = (
@@ -122,65 +195,6 @@
         send_ref[pl.ds(SEND * owner, SEND), :] = packed
 
 
-def prepare_kernel(
-    lists_ref,
-    counts_ref,
-    tiles_ref,
-    camera_ref,
-    lane_ref,
-    block_ref,
-    cast_ref,
-    column_ref,
-    places_ref,
-    chosen_ref,
-    before_ref,
-    behind_ref,
-    basis_ref,
-):
-    quarter = iota((8, 128), 0) & 3
-    fine = iota((256, 128), 0)
-    coarse = iota((32, 128), 0)
-    for group in range(GROUPS):
-        view, half = divmod(group, 2)
-        local = lists_ref[view, :, 128 * half : 128 * half + 128] & 8191
-        spread = jnp.broadcast_to(local, (8, 128))
-        lane_ref[pl.ds(8 * group, 8), :] = spread & 127
-        block_ref[pl.ds(8 * group, 8), :] = (spread >> 7) - quarter
-        lanes = pl.ds(128 * group, 128)
-        places_ref[:, lanes] = jnp.where((local & 255) == fine, 1.0, 0.0).astype(bf16)
-        owner_part = ((local >> 8) & 1) * 16 + (local >> 9)
-        chosen_ref[:, lanes] = jnp.where(owner_part == coarse, 1.0, 0.0).astype(bf16)
-    for i in range(8):
-        cast_ref[pl.ds(8 * i, GROUPS), :] = per_view(
-            [camera_ref[view, i] for view in range(VIEWS)]
-        )
-    place = iota((GROUPS, 128), 0)
-    position = (place & 1) * 128 + iota((GROUPS, 128), 1)
-    live = position < per_view([counts_ref[view, 0] for view in range(VIEWS)])
-    cast_ref[pl.ds(64, GROUPS), :] = jnp.where(live, 1.0, 0.0)
-    tile = per_view([tiles_ref[view, 0] for view in range(VIEWS)])
-    cast_ref[pl.ds(72, GROUPS), :] = (tile % TILES_WIDE * 16 + 8).astype(f32)
-    cast_ref[pl.ds(80, GROUPS), :] = (tile // TILES_WIDE * 16 + 8).astype(f32)
-    for view in range(VIEWS):
-        for half, column in enumerate(harmonic_halves(camera_ref, view)):
-            column_ref[pl.ds(16 * view + 8 * half, 8), :] = column
-    first = iota((256, 256), 0)
-    second = iota((256, 256), 1)
-    for ref, strictly in ((before_ref, first < second), (behind_ref, first > second)):
-        ones = jnp.where(strictly, 1.0, 0.0).astype(bf16)
-        ref[0:256, :] = ones
-        ref[256:512, :] = ones
-    pixel = iota((16, 256), 1)
-    power = iota((16, 256), 0)
-    pixel_u = (pixel % 16).astype(f32) - 7.5
-    pixel_v = (pixel // 16).astype(f32) - 7.5
-    basis = jnp.where(power == 0, 1.0, jnp.where(power == 1, pixel_u, pixel_v))
-    basis = jnp.where(power == 3, pixel_u * pixel_u, basis)
-    basis = jnp.where(power == 4, pixel_u * pixel_v, basis)
-    basis = jnp.where(power == 5, pixel_v * pixel_v, basis)
-    basis_ref[...] = jnp.where(power > 5, 0.0, basis).astype(bf16)
-
-
 def split(value):
     high = value.astype(bf16)
     return high, (value - high.astype(f32)).astype(bf16)
@@ -204,7 +218,7 @@
     block_ref,
     cast_ref,
     before_ref,
-    target_ref,
+    target_hbm,
     image_ref,
     loss_ref,
     shade_ref,
@@ -219,7 +233,11 @@
     logs_ref,
     high_ref,
     low_ref,
+    target_ref,
+    sem,
 ):
+    goal = pltpu.make_async_copy(target_hbm, target_ref, sem.at[0])
+    goal.start()
     for group in range(GROUPS):
         view, half = divmod(group, 2)
         lane = lane_ref[pl.ds(8 * group, 8), :]
@@ -301,6 +319,7 @@
                 pl.ds(8 * n + half, VIEWS, stride=2), :
             ]
 
+    goal.wait()
     offset = iota((16, 256), 0).astype(f32) - 7.5
     losses = jnp.zeros((8, 128), f32)
 
@@ -378,12 +397,23 @@
     cast_ref,
     behind_ref,
     basis_ref,
+    moment_one_hbm,
+    moment_two_hbm,
     grads_ref,
+    moment_one_ref,
+    moment_two_ref,
     logs_ref,
     high_ref,
     low_ref,
     moment_ref,
+    sems,
 ):
+    copies = [
+        pltpu.make_async_copy(moment_one_hbm, moment_one_ref, sems.at[0]),
+        pltpu.make_async_copy(moment_two_hbm, moment_two_ref, sems.at[1]),
+    ]
+    for copy in copies:
+        copy.start()
     basis = basis_ref[...]
 
     for view in range(VIEWS):
@@ -485,6 +515,8 @@
         high = value.astype(bf16).astype(f32)
         grads_ref[pl.ds(16 * n, GROUPS), :] = high
         grads_ref[pl.ds(16 * n + 8, GROUPS), :] = value - high
+    for copy in copies:
+        copy.wait()
 
 
 def scatter_kernel(
@@ -493,9 +525,9 @@
     grads_ref,
     tint_ref,
     loss_ref,
-    core_ref,
     side_ref,
-    across_ref,
+    far_ref,
+    wrap_ref,
     back_ref,
     spread_ref,
 ):
@@ -518,7 +550,7 @@
                     chosen * jnp.broadcast_to(piece, (32, 128)).astype(bf16)
                 )
 
-    losses = (loss_ref[...] + core_ref[...]) + (side_ref[...] + across_ref[...])
+    losses = (loss_ref[...] + side_ref[...]) + (far_ref[...] + wrap_ref[...])
 
     def store(row, value):
         for upper in range(2):
@@ -643,29 +675,25 @@
 
 
 def shards(params, moment_one, moment_two, camera, target, tile_ids, splat_lists, counts):
-    sent, slope = pl.pallas_call(
+    wide = shape(59, 512)
+    (
+        sent,
+        slope,
+        lane,
+        block,
+        cast,
+        column,
+        places,
+        chosen,
+        before,
+        behind,
+        basis,
+        params,
+    ) = pl.pallas_call(
         pack_kernel,
-        out_shape=(shape(OWNERS * SEND, 128), shape(36, 128)),
-        in_specs=[HB, HB],
-        out_specs=(VM, VM),
-        scratch_shapes=[
-            pltpu.VMEM((59, 512), f32),
-            pltpu.VMEM((SEND, 128), f32),
-            pltpu.VMEM((256, 128), f32),
-            pltpu.SMEM((3, 11), f32),
-            pltpu.SemaphoreType.DMA((2,)),
-        ],
-        compiler_params=limit(4),
-        name="pack",
-    )(in_hbm(params), in_hbm(camera))
-    table = lax.all_to_all(
-        sent.reshape(OWNERS, SEND, 128), TILE, split_axis=0, concat_axis=0, tiled=True
-    ).reshape(OWNERS * SEND, 128)
-    late = lax.optimization_barrier((slope, splat_lists, counts, tile_ids, camera))
-    slope = late[0]
-    lane, block, cast, column, places, chosen, before, behind, basis = pl.pallas_call(
-        prepare_kernel,
         out_shape=(
+            shape(OWNERS * SEND, 128),
+            shape(36, 128),
             jax.ShapeDtypeStruct((48, 128), jnp.int32),
             jax.ShapeDtypeStruct((48, 128), jnp.int32),
             shape(88, 128),
@@ -675,13 +703,31 @@
             jax.ShapeDtypeStruct((512, 256), bf16),
             jax.ShapeDtypeStruct((512, 256), bf16),
             jax.ShapeDtypeStruct((16, 256), bf16),
+            wide,
         ),
-        in_specs=[VM, SM, SM, SM],
-        out_specs=(VM,) * 9,
-        compiler_params=limit(4),
-        cost_estimate=pl.CostEstimate(flops=1 << 28, bytes_accessed=1 << 20, transcendentals=0),
-        name="prepare",
-    )(*late[1:])
+        in_specs=[HB] * 5,
+        out_specs=(VM,) * 12,
+        scratch_shapes=[
+            pltpu.VMEM((SEND, 128), f32),
+            pltpu.VMEM((256, 128), f32),
+            pltpu.SMEM((3, 11), f32),
+            pltpu.VMEM((VIEWS, 1, 256), jnp.int32),
+            pltpu.SMEM((1, 3), jnp.int32),
+            pltpu.SMEM((1, 3), jnp.int32),
+            pltpu.SemaphoreType.DMA((8,)),
+        ],
+        compiler_params=limit(6),
+        name="pack",
+    )(
+        in_hbm(params),
+        in_hbm(camera),
+        in_hbm(splat_lists),
+        in_hbm(counts.reshape(1, VIEWS)),
+        in_hbm(tile_ids.reshape(1, VIEWS)),
+    )
+    table = lax.all_to_all(
+        sent.reshape(OWNERS, SEND, 128), TILE, split_axis=0, concat_axis=0, tiled=True
+    ).reshape(OWNERS * SEND, 128)
     half = jax.ShapeDtypeStruct((48, 256), bf16)
     image, loss, shade, keep, pulled, stacked, tint, entries = pl.pallas_call(
         front_kernel,
@@ -695,7 +741,7 @@
             shape(24, 256),
             shape(8 * KEPT, 128),
         ),
-        in_specs=[VM] * 6,
+        in_specs=[VM] * 5 + [HB],
         out_specs=(VM,) * 8,
         scratch_shapes=[
             pltpu.VMEM((GROUPS * SEND, 128), f32),
@@ -704,30 +750,44 @@
             pltpu.VMEM((256, 512), bf16),
             pltpu.VMEM((256, 256), bf16),
             pltpu.VMEM((256, 256), bf16),
+            pltpu.VMEM((VIEWS, 3, 1, 256), f32),
+            pltpu.SemaphoreType.DMA((1,)),
         ],
         compiler_params=limit(16),
         name="front",
-    )(table, lane, block, cast, before, target)
-    core = swapped(loss, lambda i: i ^ 1)
+    )(table, lane, block, cast, before, in_hbm(target))
     side = swapped(loss, lambda i: i ^ 2)
-    across = swapped(loss, lambda i: i ^ 3)
-    grads = pl.pallas_call(
+    far = swapped(loss, lambda i: i ^ 4)
+    wrap = swapped(loss, lambda i: i ^ 6)
+    grads, moment_one, moment_two = pl.pallas_call(
         back_kernel,
-        out_shape=shape(16 * GEOMETRY, 128),
-        in_specs=[VM] * 8,
-        out_specs=VM,
+        out_shape=(shape(16 * GEOMETRY, 128), wide, wide),
+        in_specs=[VM] * 8 + [HB] * 2,
+        out_specs=(VM,) * 3,
         scratch_shapes=[
             pltpu.VMEM((256, 512), bf16),
             pltpu.VMEM((256, 256), bf16),
             pltpu.VMEM((256, 256), bf16),
             pltpu.VMEM((64, 128), f32),
+            pltpu.SemaphoreType.DMA((2,)),
         ],
         compiler_params=limit(12),
         cost_estimate=pl.CostEstimate(
             flops=1 << 31, bytes_accessed=1 << 23, transcendentals=1 << 20
         ),
         name="back",
-    )(shade, keep, pulled, stacked, entries, cast, behind, basis)
+    )(
+        shade,
+        keep,
+        pulled,
+        stacked,
+        entries,
+        cast,
+        behind,
+        basis,
+        in_hbm(moment_one),
+        in_hbm(moment_two),
+    )
     back = pl.pallas_call(
         scatter_kernel,
         out_shape=shape(OWNERS * SEND, 128),
@@ -736,7 +796,7 @@
         scratch_shapes=[pltpu.VMEM((2 * 32 * GEOMETRY + 192, 768), bf16)],
         compiler_params=limit(12),
         name="scatter",
-    )(places, chosen, grads, tint, loss, core, side, across)
+    )(places, chosen, grads, tint, loss, side, far, wrap)
     arrived = lax.all_to_all(
         back.reshape(OWNERS, SEND, 128), TILE, split_axis=0, concat_axis=0, tiled=True
     ).reshape(OWNERS * SEND, 128)
@@ -748,8 +808,7 @@
         compiler_params=limit(4),
         name="fold",
     )(arrived)
-    other = swapped(loss, lambda i: 6 - (i & 6) + (i & 1))
-    wide = shape(59, 512)
+    core = swapped(loss, lambda i: i ^ 1)
     updated, first, second, rendered = pl.pallas_call(
         adam_kernel,
         out_shape=(wide, wide, wide, shape(VIEWS, 3, 1, 256)),
@@ -769,7 +828,7 @@
         ),
         name="adam",
     )(total, slope, column, image, params, moment_one, moment_two)
-    losses = (loss + other)[4, :VIEWS] * (0.5 / (3 * 256 * 128))
+    losses = (loss + core)[4, :VIEWS] * (0.5 / (3 * 256 * 128))
     return (updated, first, second, rendered, losses)
 
 

time: 53.2 us -> 51.4 us (0.966)
  the two profiles are of different devices: /device:TPU:0 before, /device:TPU:1 now
where the time goes in v3:
time: 51.4 us; the launch traced here: 51.1 us
  blocking collectives  32.9 us (64%)
  starting transfers between devices  8.04 us (16%)
  Pallas kernels  7 us (14%)
  waiting for transfers between devices  1.88 us (4%)
  between operations  0.7 us (1%)
  other arithmetic  0.52 us (1%)
    all_to_all x1, blocking collectives, shards(): lax.all_to_all(sent.reshape(OWNERS, SEND, 128), TILE, split_axis=0, conca...  20.1 us
    all_to_all x1, blocking collectives, shards(): lax.all_to_all(back.reshape(OWNERS, SEND, 128), TILE, split_axis=0, conca...  12.9 us
    ppermute x4, starting transfers between devices, swapped(): return lax.ppermute(value, GAUSS, [(i, partner(i)) for i in range(8)])  8.04 us
    pallas_call x1, Pallas kernels, shards(): pl.pallas_call(front_kernel, out_shape=(shape(16, 256), shape(8, 128), sh...  2.94 us
    ppermute x4, waiting for transfers between devices, swapped(): return lax.ppermute(value, GAUSS, [(i, partner(i)) for i in range(8)])  1.88 us
    pallas_call x1, Pallas kernels, shards(): pl.pallas_call(back_kernel, out_shape=(shape(16 * GEOMETRY, 128), wide, w...  1.4 us
    pallas_call x1, Pallas kernels, shards(): pl.pallas_call(pack_kernel, out_shape=(shape(OWNERS * SEND, 128), shape(3...  1.06 us
  transfers between devices with their start and end apart: 4, of which 1 were waited for; matrix products, arithmetic and copies ran while one was open for 0% of the time, Pallas kernels for 5%

profile of v3, /device:TPU:1, one launch (start us, length us, event | category | flops | bytes accessed | tf_op | source)
XLA Modules:
  0.0 51.1 jit_solution(15638108530453956452)
XLA Ops:
  0.6 1.1 %pack.1 = (f32[1280,128]{1,0:T(8,128)S(1)}, f32[36,128]{1,0:T(8,128)S(1)}, s32[48,128]{1,0:T(8,128)S(1)}, s32[48,128]{1,0:T(8,128)S(1)}, f32[88,128]{1,0:T(8,128...) custom-call(f32[59,512]{1,0:T(8,128)} %params_hbm.1, ...), custom_call_target="tpu_custom_call" | custom-call | tf_op jit(solution)/shard_map/pack/pallas_call | solution.py:692
  1.7 20.1 %all_to_all.10 = f32[16,80,128]{2,1,0:T(8,128)S(1)} all-to-all(f32[16,80,128]{2,1,0:T(8,128)S(1)} %bitcast.11), channel_id=1, replica_groups=mesh['gauss_0'=4,'gauss_1'=2,'tile_0'=4,'tile_1'=4] {'tile_0','tile_1'}, dimensions={0} | all-to-all | bytes 1310720 | tf_op jit(solution)/shard_map/all_to_all | solution.py:728
  21.8 2.9 %front.1 = (f32[16,256]{1,0:T(8,128)S(1)}, f32[8,128]{1,0:T(8,128)S(1)}, f32[768,256]{1,0:T(8,128)S(1)}, f32[768,256]{1,0:T(8,128)S(1)}, bf16[48,256]{1,0:T(8,12...) custom-call(f32[1280,128]{1,0:T(8,128)S(1)} %bitcast.8, ...), custom_call_target="tpu_custom_call" | custom-call | tf_op jit(solution)/shard_map/front/pallas_call | solution.py:732
  24.7 2.8 %collective-permute-start.2 = (f32[8,128]{1,0:T(8,128)S(1)}, f32[8,128]{1,0:T(8,128)S(1)}, u32[]{:S(2)}, u32[]{:S(2)}) collective-permute-start(f32[8,128]{1,0:T(8,128)S(1)} %get-tuple-element.50.loss_ref), channel_id=1, source_target_pairs={{0,96},{16,112},{32,64},{48,80},{64,32},{80,48},{96,0},{112,16},{1... | collective-permute-start | bytes 12296 | tf_op jit(solution)/shard_map/ppermute | solution.py:666
  27.5 0.4 collective-permute-start.1
  27.9 0.3 collective-permute-start
  28.2 1.4 %back.1 = (f32[160,128]{1,0:T(8,128)S(1)}, f32[59,512]{1,0:T(8,128)S(1)}, f32[59,512]{1,0:T(8,128)S(1)}) custom-call(f32[768,256]{1,0:T(8,128)S(1)} %get-tuple-element.41.shade_ref, f32[768,256]{1,0:T(8,128)S(1)} %get-tuple-element.42.keep_ref, bf16[48,256]{1,0:T(8,128)(2,1)S(1)} %get-tuple-element.43.pulled_ref, ...), custom_call_target="tpu_custom_call" | custom-call | flops 2147483648 | bytes 8388608 | tf_op jit(solution)/shard_map/back/pallas_call | solution.py:762
  29.6 0.0 collective-permute-done.2.wrap_ref
  29.6 1.9 %collective-permute-done.1.far_ref = f32[8,128]{1,0:T(8,128)S(1)} collective-permute-done((f32[8,128]{1,0:T(8,128)S(1)}, f32[8,128]{1,0:T(8,128)S(1)}, u32[]{:S(2)}, u32[]{:S(2)}) %collective-permute-start.1) | collective-permute-done | bytes 4128 | tf_op jit(solution)/shard_map/ppermute | solution.py:666
  31.5 0.0 collective-permute-done.side_ref
  31.5 0.7 %scatter.1 = f32[1280,128]{1,0:T(8,128)S(1)} custom-call(bf16[256,768]{1,0:T(8,128)(2,1)S(1)} %get-tuple-element.34.places_ref, bf16[32,768]{1,0:T(8,128)(2,1)S(1)} %get-tuple-element.35.chosen_ref, f32[160,128]{1,0:T(8,128)S(1)} %get-tuple-element.48.grads_ref, f32[24,256]{1,0:T(8,128)S(1)} %get-tuple-element.49.tint_ref, ...), custom_call_target="tpu_custom_call" | custom-call | tf_op jit(solution)/shard_map/scatter/pallas_call | solution.py:791
  32.2 12.9 %all_to_all.11 = f32[16,80,128]{2,1,0:T(8,128)S(1)} all-to-all(f32[16,80,128]{2,1,0:T(8,128)S(1)} %bitcast.9), channel_id=1, replica_groups=mesh['gauss_0'=4,'gauss_1'=2,'tile_0'=4,'tile_1'=4] {'tile_0','tile_1'}, dimensions={0} | all-to-all | bytes 1310720 | tf_op jit(solution)/shard_map/all_to_all | solution.py:800
  45.1 4.6 %collective-permute-start.3 = (f32[8,128]{1,0:T(8,128)S(1)}, f32[8,128]{1,0:T(8,128)S(1)}, u32[]{:S(2)}, u32[]{:S(2)}) collective-permute-start(f32[8,128]{1,0:T(8,128)S(1)} %get-tuple-element.62), channel_id=1, source_target_pairs={{0,16},{16,0},{32,48},{48,32},{64,80},{80,64},{96,112},{112,96},{1... | collective-permute-start | bytes 12296 | tf_op jit(solution)/shard_map/ppermute | solution.py:666
  49.6 0.9 %adam.1 = (f32[59,512]{1,0:T(8,128)}, f32[59,512]{1,0:T(8,128)}, f32[59,512]{1,0:T(8,128)}, f32[3,3,1,256]{3,2,1,0:T(1,128)}) custom-call(f32[80,128]{1,0:T(8,128)S(1)} %get-tuple-element.51.total_ref, f32[36,128]{1,0:T(8,128)S(1)} %get-tuple-element.52.slope_ref, f32[48,128]{1,0:T(8,128)S(1)} %get-tuple-element.53.column_ref, ...), custom_call_target="tpu_custom_call" | custom-call | flops 1073741824 | bytes 4194304 | tf_op jit(solution)/shard_map/adam/pallas_call | solution.py:812
  50.5 0.0 collective-permute-done.3
  50.6 0.5 %multiply_bitcast_fusion = f32[3]{0:T(128)} fusion(f32[8,128]{1,0:T(8,128)S(1)} %add.3), kind=kLoop, calls=%fused_computation | loop fusion | flops 3 | bytes 24 | tf_op jit(solution)/shard_map/mul | solution.py:831
  (2 shorter events, 0.0 us)
Async XLA Ops:
  24.7 4.9 %collective-permute-start.2 = (f32[8,128]{1,0:T(8,128)S(1)}, f32[8,128]{1,0:T(8,128)S(1)}, u32[]{:S(2)}, u32[]{:S(2)}) collective-permute-start(f32[8,128]{1,0:T(8,128)S(1)} %get-tuple-element.50.loss_ref), channel_id=1, source_target_pairs={{0,96},{16,112},{32,64},{48,80},{64,32},{80,48},{96,0},{112,16},{1... | collective-permute-start | bytes 12296 | tf_op jit(solution)/shard_map/ppermute | solution.py:666
  27.5 4.0 %collective-permute-start.1 = (f32[8,128]{1,0:T(8,128)S(1)}, f32[8,128]{1,0:T(8,128)S(1)}, u32[]{:S(2)}, u32[]{:S(2)}) collective-permute-start(f32[8,128]{1,0:T(8,128)S(1)} %get-tuple-element.50.loss_ref), channel_id=1, source_target_pairs={{0,64},{16,80},{32,96},{48,112},{64,0},{80,16},{96,32},{112,48},{1... | collective-permute-start | bytes 12296 | tf_op jit(solution)/shard_map/ppermute | solution.py:666
  27.9 3.6 %collective-permute-start = (f32[8,128]{1,0:T(8,128)S(1)}, f32[8,128]{1,0:T(8,128)S(1)}, u32[]{:S(2)}, u32[]{:S(2)}) collective-permute-start(f32[8,128]{1,0:T(8,128)S(1)} %get-tuple-element.50.loss_ref), channel_id=1, source_target_pairs={{0,32},{16,48},{32,0},{48,16},{64,96},{80,112},{96,64},{112,80},{1... | collective-permute-start | bytes 12296 | tf_op jit(solution)/shard_map/ppermute | solution.py:666
  45.1 5.5 %collective-permute-start.3 = (f32[8,128]{1,0:T(8,128)S(1)}, f32[8,128]{1,0:T(8,128)S(1)}, u32[]{:S(2)}, u32[]{:S(2)}) collective-permute-start(f32[8,128]{1,0:T(8,128)S(1)} %get-tuple-element.62), channel_id=1, source_target_pairs={{0,16},{16,0},{32,48},{48,32},{64,80},{80,64},{96,112},{112,96},{1... | collective-permute-start | bytes 12296 | tf_op jit(solution)/shard_map/ppermute | solution.py:666
